TPU v7x, 32 devices: a whole 2x2x4 slice. The times are simulated.
32 devices in a mesh: parts: 2 (over x), seq: 16 (over z, y, core).
Axes of the slice: x: 2, y: 2, z: 4, core: 2. Of those that a mesh axis runs over, the one named last changes fastest.
Arguments:
- queries: bfloat16 [2, 4, 8192], P(None, 'parts'), parts along dimension 1, may hold values from -7 to 7
- cache_k: bfloat16 [65536, 1024], P(('parts', 'seq')), parts along dimension 0, may hold values from -15 to 15
- cache_v: bfloat16 [65536, 1024], P(('parts', 'seq')), parts along dimension 0, may hold values from -6 to 6
- context_len: int32 [4], P('parts'), parts along dimension 0, may hold values from 8192 to 16384, as said below
- slot_seq: int32 [65536], P(('parts', 'seq')), parts along dimension 0, may hold values from 0 to 2, as said below
- slot_pos: int32 [65536], P(('parts', 'seq')), parts along dimension 0, may hold values from 0 to 16383, as said below
Outputs:
- attended: bfloat16 [2, 4, 8192], P(None, 'parts'), parts along dimension 1
There are 2 independent parts, one for each index of `parts`. A program takes and returns all parts, laid end to end along the dimension named above; each array names one. Nothing has to cross between parts.
Inputs may be any that keep to these rules, and one draw needn't show every extreme that they name: Each sequence s has exactly context_len[s] slots with slot_seq = s; some sequence has exactly 16384. `slot_seq`: aligned blocks of 128 slots belong to one sequence or are free; the slots of a sequence hold each position from 0 to context_len[s] - 1 exactly once; free slots carry 2. `slot_pos`: 0 on free slots.
All inputs are finite; a program needn't handle non-finite values.
Results may differ from a plain program's by a relative error of at most 0.006.
Values may be sent and summed in bfloat16 or wider, within the bound.
A program may use at most 64 MiB of HBM per device.

v0:
```python
import functools

import jax
import jax.numpy as jnp
from jax import lax
from jax.experimental import pallas as pl
from jax.experimental.pallas import tpu as pltpu
from jax.sharding import PartitionSpec as P

KVH = 8
HD = 128
INNER = 4
LIMIT = 16 << 20
SHIFT = HD ** (-0.5) * 1.4426950408889634
HIDDEN = -1e30
MESH = pl.DeviceIdType.MESH


def rows_to_columns(rows):
    return jnp.transpose(rows)


def scaled_sum(ml, numer_refs, count, rows, final):
    maxima = [ml(i)[0:1, :] for i in range(count)]
    denoms = [ml(i)[1:2, :] for i in range(count)]
    top = functools.reduce(jnp.maximum, maxima)
    factors = [jnp.exp2((m - top) * SHIFT) for m in maxima]
    denom = sum(f * d for f, d in zip(factors, denoms))
    if final:
        factors = [f / denom for f in factors]
    pad = -count % 8
    if pad:
        factors = factors + [jnp.zeros((pad, 128), jnp.float32)]
    columns = jnp.transpose(jnp.concatenate(factors, axis=0))
    numer = None
    for i in range(count):
        term = numer_refs(i) * columns[:rows, i : i + 1]
        numer = term if numer is None else numer + term
    return top, denom, numer


def kernel(
    n, ctx_hbm, q_hbm, k_hbm, v_hbm, seq_hbm, pos_hbm, fin,
    ctx, q_ref, seq_ref, pos_ref, kbuf, vbuf, qf, bias,
    num1, ml1, rnum1, rml1, num2, ml2, rnum2, rml2, own,
    isem, ksem, vsem, s1, s1m, r1, r1m, s2, s2m, r2, r2m, s3, r3,
):
    me = lax.axis_index("seq")
    outer_count = n // INNER
    inner = me % INNER
    outer = me // INNER
    y = inner // 2
    c = inner % 2
    owners = [inner, y * 2 + (1 - c), (1 - y) * 2 + c, (1 - y) * 2 + (1 - c)]
    heads_each = KVH // INNER
    width = heads_each * HD
    rows = q_ref.shape[0] * q_ref.shape[1] * (q_ref.shape[2] // HD // KVH)
    group = q_ref.shape[2] // HD // KVH
    seqs = q_ref.shape[1]
    block = heads_each * rows

    barrier = pltpu.get_barrier_semaphore()
    plane_peers = {j: outer * INNER + owners[j] for j in (1, 2, 3)}
    chain_peers = {k: ((outer + k) % outer_count) * INNER + inner for k in range(1, outer_count)}
    peers = list(plane_peers.values()) + list(chain_peers.values())
    for peer in peers:
        pl.semaphore_signal(barrier, inc=1, device_id={"seq": peer}, device_id_type=MESH)

    inputs = []
    for i, (src, dst) in enumerate(((q_hbm, q_ref), (seq_hbm, seq_ref), (pos_hbm, pos_ref), (ctx_hbm, ctx))):
        copy = pltpu.make_async_copy(src, dst, isem.at[i])
        copy.start()
        inputs.append(copy)
    kcopies, vcopies = {}, {}
    for which, j in (("k", 2), ("k", 3), ("v", 2), ("k", 1), ("v", 3), ("k", 0), ("v", 1), ("v", 0)):
        columns = pl.ds(pl.multiple_of(owners[j] * width, width), width)
        src, dst, sem, kept = (k_hbm, kbuf, ksem, kcopies) if which == "k" else (v_hbm, vbuf, vsem, vcopies)
        kept[j] = pltpu.make_async_copy(src.at[:, columns], dst.at[j], sem.at[j])
        kept[j].start()

    for copy in inputs:
        copy.wait()

    for t in range(2):
        for head in range(KVH * group):
            g, h = head // group, head % group
            base = g * rows + t * group * seqs + h * seqs
            qf[base : base + seqs, :] = q_ref[t, :, head * HD : (head + 1) * HD].astype(jnp.float32)

    slots = k_hbm.shape[0]
    row_ids = lax.broadcasted_iota(jnp.int32, (rows, 128), 0)
    row_seq = row_ids % seqs
    row_step = row_ids // (group * seqs)
    last = jnp.zeros((rows, 128), jnp.int32)
    for s in range(seqs):
        last = jnp.where(row_seq == s, ctx[s], last)
    last = last - 2 + row_step
    for b in range(slots // 128):
        cut = slice(b * 128, (b + 1) * 128)
        owner = jnp.broadcast_to(seq_ref[:, cut], (rows, 128))
        pos = jnp.broadcast_to(pos_ref[:, cut], (rows, 128))
        allowed = (owner == row_seq) & (pos <= last)
        bias[:, cut] = jnp.where(allowed, 0.0, HIDDEN)

    copies1 = []
    waiting = {}
    lane = lax.broadcasted_iota(jnp.int32, (rows, 128), 1)

    def score(j):
        kcopies[j].wait()
        probs = []
        packed = []
        for e in range(heads_each):
            start = pl.multiple_of((owners[j] * heads_each + e) * rows, rows)
            q = qf[pl.ds(start, rows), :].astype(jnp.bfloat16)
            scores = lax.dot_general(
                q, kbuf[j, :, e * HD : (e + 1) * HD], (((1,), (1,)), ((), ())),
                preferred_element_type=jnp.float32,
            ) + bias[...]
            m = jnp.max(scores, axis=-1, keepdims=True)
            w = jnp.exp2((scores - m) * SHIFT)
            l = jnp.sum(w, axis=-1, keepdims=True)
            probs.append(w.astype(jnp.bfloat16))
            packed.append(jnp.where(lane == 0, m, l))
        packed = packed + [jnp.zeros((128 - block, 128), jnp.float32)]
        ml1[j] = jnp.transpose(jnp.concatenate(packed, axis=0))[:2, :]
        waiting[j] = probs

    def send1(src, dst, ss, rs, j):
        copy = pltpu.make_async_remote_copy(
            src_ref=src.at[j], dst_ref=dst.at[j], send_sem=ss.at[j], recv_sem=rs.at[j],
            device_id={"seq": plane_peers[j]}, device_id_type=MESH,
        )
        copy.start()
        copies1.append(copy)

    def gather(j):
        vcopies[j].wait()
        for e in range(heads_each):
            num1[j, e * rows : (e + 1) * rows, :] = jnp.dot(
                waiting[j][e], vbuf[j, :, e * HD : (e + 1) * HD], preferred_element_type=jnp.float32
            ).astype(jnp.bfloat16)
        if j:
            if j == 2:
                pl.semaphore_wait(barrier, len(peers))
            send1(ml1, rml1, s1m, r1m, j)
            send1(num1, rnum1, s1, r1, j)

    score(2)
    score(3)
    gather(2)
    score(1)
    gather(3)
    score(0)
    gather(1)
    gather(0)

    for copy in copies1:
        copy.wait_recv()
    top, denom, numer = scaled_sum(
        lambda i: rml1[i] if i else ml1[0],
        lambda i: (rnum1[i] if i else num1[0]).astype(jnp.float32),
        INNER, block, False,
    )
    ml2[...] = jnp.concatenate([top, denom], axis=0)
    num2[...] = numer.astype(jnp.bfloat16)

    copies2 = []
    for k in range(1, outer_count):
        for src, dst, ss, rs in ((ml2, rml2, s2m, r2m), (num2, rnum2, s2, r2)):
            copy = pltpu.make_async_remote_copy(
                src_ref=src, dst_ref=dst.at[k], send_sem=ss.at[k], recv_sem=rs.at[k],
                device_id={"seq": chain_peers[k]}, device_id_type=MESH,
            )
            copy.start()
            copies2.append(copy)
    for copy in copies2:
        copy.wait_recv()
    _, _, attended = scaled_sum(
        lambda i: rml2[i] if i else ml2[...],
        lambda i: (rnum2[i] if i else num2[...]).astype(jnp.float32),
        outer_count, block, True,
    )
    own[...] = attended.astype(jnp.bfloat16)

    copies3 = []
    for j in (2, 3, 1):
        copy = pltpu.make_async_remote_copy(
            src_ref=own, dst_ref=fin.at[inner], send_sem=s3.at[j], recv_sem=r3.at[j],
            device_id={"seq": plane_peers[j]}, device_id_type=MESH,
        )
        copy.start()
        copies3.append(copy)
    fin[inner] = own[...]
    for copy in copies3:
        copy.wait_recv()
    for copy in copies1 + copies2 + copies3:
        copy.wait_send()


def place(fin, out_ref):
    steps, seqs, _ = out_ref.shape
    block = fin.shape[1]
    heads = fin.shape[0] * block // (steps * seqs)
    group = heads // KVH
    for head in range(heads):
        g, h = head // group, head % group
        for t in range(steps):
            row = g * group * steps * seqs + t * group * seqs + h * seqs
            i, base = row // block, row % block
            out_ref[t, :, head * HD : (head + 1) * HD] = fin[i, base : base + seqs, :]


def per_device(n, queries, cache_k, cache_v, context_len, slot_seq, slot_pos):
    slots = cache_k.shape[0]
    seqs = queries.shape[1]
    heads = queries.shape[2] // HD
    rows = 2 * seqs * heads // KVH
    heads_each = KVH // INNER
    block = heads_each * rows
    outer = n // INNER
    vmem = pl.BlockSpec(memory_space=pltpu.VMEM)
    dma = pltpu.SemaphoreType.DMA
    anywhere = pl.BlockSpec(memory_space=pltpu.HBM)
    attended = pl.pallas_call(
        functools.partial(kernel, n),
        out_shape=jax.ShapeDtypeStruct((INNER, block, HD), jnp.bfloat16),
        in_specs=[anywhere] * 6,
        out_specs=vmem,
        scratch_shapes=[
            pltpu.SMEM((seqs,), jnp.int32),
            pltpu.VMEM(queries.shape, jnp.bfloat16),
            pltpu.VMEM((1, slots), jnp.int32),
            pltpu.VMEM((1, slots), jnp.int32),
            pltpu.VMEM((INNER, slots, heads_each * HD), jnp.bfloat16),
            pltpu.VMEM((INNER, slots, heads_each * HD), jnp.bfloat16),
            pltpu.VMEM((KVH * rows, HD), jnp.float32),
            pltpu.VMEM((rows, slots), jnp.float32),
            pltpu.VMEM((INNER, block, HD), jnp.bfloat16),
            pltpu.VMEM((INNER, 2, 128), jnp.float32),
            pltpu.VMEM((INNER, block, HD), jnp.bfloat16),
            pltpu.VMEM((INNER, 2, 128), jnp.float32),
            pltpu.VMEM((block, HD), jnp.bfloat16),
            pltpu.VMEM((2, 128), jnp.float32),
            pltpu.VMEM((outer, block, HD), jnp.bfloat16),
            pltpu.VMEM((outer, 2, 128), jnp.float32),
            pltpu.VMEM((block, HD), jnp.bfloat16),
            dma((4,)), dma((INNER,)), dma((INNER,)),
            dma((INNER,)), dma((INNER,)), dma((INNER,)), dma((INNER,)),
            dma((outer,)), dma((outer,)), dma((outer,)), dma((outer,)),
            dma((INNER,)), dma((INNER,)),
        ],
        compiler_params=pltpu.CompilerParams(collective_id=0, has_side_effects=True, vmem_limit_bytes=LIMIT),
    )(*[
        pltpu.with_memory_space_constraint(x, pltpu.HBM)
        for x in (context_len, queries, cache_k, cache_v, slot_seq.reshape(1, slots), slot_pos.reshape(1, slots))
    ])
    return pl.pallas_call(
        place,
        out_shape=jax.ShapeDtypeStruct(queries.shape, jnp.bfloat16),
        in_specs=[vmem],
        out_specs=vmem,
        compiler_params=pltpu.CompilerParams(vmem_limit_bytes=4 << 20),
    )(attended)


def solution(mesh):
    return jax.shard_map(
        functools.partial(per_device, mesh.shape["seq"]),
        mesh=mesh,
        in_specs=(
            P(None, "parts", None),
            P(("parts", "seq"), None),
            P(("parts", "seq"), None),
            P("parts"),
            P(("parts", "seq")),
            P(("parts", "seq")),
        ),
        out_specs=P(None, "parts", None),
        check_vma=False,
    )
```

profile of v0, /device:TPU:0, one launch (start us, length us, event | category | flops | bytes accessed | tf_op | source)
XLA Modules:
  0.0 18.3 jit_solution(1555858796231576557)
XLA Ops:
  0.0 17.6 %shard_map.64.fin = bf16[4,64,128]{2,1,0:T(8,128)(2,1)S(1)} custom-call(s32[2]{0:T(128)} %ctx_hbm.1, bf16[2,2,8192]{2,1,0:T(2,128)(2,1)} %q_hbm.1, bf16[2048,1024]{1,0:T(8,128)(2,1)} %k_hbm.1, bf16[2048,1024]{1,0:T(8,128)(2,1)} %v_hbm.1, s32[1,2048]{1,0:T(1,128)} %bitcast.2, s32[1,2048]{1,0:T(1,128)} %bitcast.3), custom_call_target="tpu_custom_call" | custom-call | tf_op jit(solution)/shard_map/pallas_call | solution.py:225
  17.6 0.7 %shard_map.65 = bf16[2,2,8192]{2,1,0:T(2,128)(2,1)} custom-call(bf16[4,64,128]{2,1,0:T(8,128)(2,1)S(1)} %shard_map.64.fin), custom_call_target="tpu_custom_call" | custom-call | tf_op jit(solution)/shard_map/pallas_call | solution.py:258
where the time goes:
time: 18.4 us; the launch traced here: 18.3 us
  Pallas kernels  18.3 us (99%)
    pallas_call x1, Pallas kernels, per_device(): pl.pallas_call(functools.partial(kernel, n), out_shape=jax.ShapeDtypeStru...  17.6 us
    pallas_call x1, Pallas kernels, per_device(): pl.pallas_call(place, out_shape=jax.ShapeDtypeStruct(queries.shape, jnp.b...  0.71 us

commit v1 on v0

v1 whole, which is shorter than its diff:
```python
import functools

import jax
import jax.numpy as jnp
from jax import lax
from jax.experimental import pallas as pl
from jax.experimental.pallas import tpu as pltpu
from jax.sharding import PartitionSpec as P

KVH = 8
HD = 128
CHUNKS = 4
PER_CORE = CHUNKS // 2
LIMIT = 20 << 20
SHIFT = HD ** (-0.5) * 1.4426950408889634
HIDDEN = -1e30
MESH = pl.DeviceIdType.MESH


def served_by(plane, planes):
    return (planes // 2) * ((4 * plane // planes + 2) // 3)


def root_planes(planes):
    return (0, planes // 2) if planes > 1 else (0,)


def kernel(
    n, ctx_hbm, q_hbm, k_hbm, v_hbm, seq_hbm, pos_hbm, out,
    ctx, q_ref, seq_ref, pos_ref, kbuf, vbuf, qf, bias,
    half_num, half_ml, peer_num, peer_ml, chip_num, chip_ml,
    isem, ksem, vsem, hs, hsm, hr, hrm, cs, csm, cr, crm, ps, pr, fs, fr,
):
    me = lax.axis_index("seq")
    chips = n // 2
    planes = chips // 2
    core = me % 2
    chip = me // 2
    y = chip % 2
    plane = chip // 2
    roots = root_planes(planes)
    is_root = functools.reduce(lambda a, b: a | b, [plane == r for r in roots])
    partner = chip * 2 + (1 - core)
    server = served_by(plane, planes) * 2 + y
    guests = {r: [p for p in range(planes) if p not in roots and served_by(p, planes) == r] for r in roots}
    heads_each = KVH // CHUNKS
    width = heads_each * HD
    group = q_ref.shape[2] // HD // KVH
    seqs = q_ref.shape[1]
    rows = 2 * seqs * group
    block = heads_each * rows
    tile = group * seqs
    span = heads_each * tile

    barrier = pltpu.get_barrier_semaphore()

    def greet(device):
        pl.semaphore_signal(barrier, inc=1, device_id={"seq": device}, device_id_type=MESH)

    inputs = []
    for i, (src, dst) in enumerate(((q_hbm, q_ref), (seq_hbm, seq_ref), (pos_hbm, pos_ref), (ctx_hbm, ctx))):
        copy = pltpu.make_async_copy(src, dst, isem.at[i])
        copy.start()
        inputs.append(copy)

    def kv(i):
        first = pl.multiple_of(((1 - core) * PER_CORE + i) % CHUNKS * width, width)
        columns = pl.ds(first, width)
        return (
            lambda: pltpu.make_async_copy(k_hbm.at[:, columns], kbuf.at[i], ksem.at[i]),
            lambda: pltpu.make_async_copy(v_hbm.at[:, columns], vbuf.at[i], vsem.at[i]),
        )

    def load(i, carry):
        for copy in kv(i):
            copy().start()
        return carry

    lax.fori_loop(0, CHUNKS, load, 0)

    greet(partner)

    @pl.when(is_root)
    def _():
        for k in range(1, chips):
            greet((chip + k) % chips * 2 + core)

    @pl.when(jnp.logical_not(is_root))
    def _():
        for d in range(2):
            greet(server * 2 + d)

    for copy in inputs:
        copy.wait()

    for t in range(2):
        for head in range(KVH * group):
            g, h = head // group, head % group
            base = g * rows + t * group * seqs + h * seqs
            qf[base : base + seqs, :] = q_ref[t, :, head * HD : (head + 1) * HD].astype(jnp.float32)

    slots = k_hbm.shape[0]
    row_ids = lax.broadcasted_iota(jnp.int32, (rows, 128), 0)
    row_seq = row_ids % seqs
    row_step = row_ids // (group * seqs)
    last = jnp.zeros((rows, 128), jnp.int32)
    for s in range(seqs):
        last = jnp.where(row_seq == s, ctx[s], last)
    last = last - 2 + row_step
    for b in range(slots // 128):
        cut = slice(b * 128, (b + 1) * 128)
        owner = jnp.broadcast_to(seq_ref[:, cut], (rows, 128))
        pos = jnp.broadcast_to(pos_ref[:, cut], (rows, 128))
        allowed = (owner == row_seq) & (pos <= last)
        bias[:, cut] = jnp.where(allowed, 0.0, HIDDEN)

    lane = lax.broadcasted_iota(jnp.int32, (rows, 128), 1)

    def score(i):
        kv(i)[0]().wait()
        probs = []
        packed = []
        for e in range(heads_each):
            head = ((1 - core) * PER_CORE + i) % CHUNKS * heads_each + e
            q = qf[pl.ds(pl.multiple_of(head * rows, rows), rows), :].astype(jnp.bfloat16)
            scores = lax.dot_general(
                q, kbuf[i, :, e * HD : (e + 1) * HD], (((1,), (1,)), ((), ())),
                preferred_element_type=jnp.float32,
            ) + bias[...]
            m = jnp.max(scores, axis=-1, keepdims=True)
            w = jnp.exp2((scores - m) * SHIFT)
            l = jnp.sum(w, axis=-1, keepdims=True)
            probs.append(w.astype(jnp.bfloat16))
            packed.append(jnp.where(lane == 0, m, l))
        packed = packed + [jnp.zeros((128 - block, 128), jnp.float32)]
        return probs, jnp.transpose(jnp.concatenate(packed, axis=0))[:2, :]

    def gather(i, probs):
        kv(i)[1]().wait()
        return jnp.concatenate(
            [
                jnp.dot(probs[e], vbuf[i, :, e * HD : (e + 1) * HD], preferred_element_type=jnp.float32)
                for e in range(heads_each)
            ],
            axis=0,
        )

    def remote(src, dst, ss, rs, device):
        return pltpu.make_async_remote_copy(
            src_ref=src, dst_ref=dst, send_sem=ss, recv_sem=rs, device_id={"seq": device}, device_id_type=MESH
        )

    def to_partner(j):
        return (
            remote(half_ml.at[j], peer_ml.at[j], hsm.at[j], hrm.at[j], partner),
            remote(half_num.at[j], peer_num.at[j], hs.at[j], hr.at[j], partner),
        )

    targets = [r * 2 + side for r in roots for side in range(2)]

    def to_root(j, i):
        device = targets[i] * 2 + core
        return (
            remote(chip_ml.at[j, chip], chip_ml.at[j, chip], csm.at[j, i], crm.at[j, chip], device),
            remote(chip_num.at[j, chip], chip_num.at[j, chip], cs.at[j, i], cr.at[j, chip], device),
        )

    def from_chip(j, k):
        slot = (chip + k) % chips
        return (
            remote(chip_ml.at[j, slot], chip_ml.at[j, slot], csm.at[j, 0], crm.at[j, slot], slot * 2 + core),
            remote(chip_num.at[j, slot], chip_num.at[j, slot], cs.at[j, 0], cr.at[j, slot], slot * 2 + core),
        )

    def part(owner, j):
        return out.at[:, pl.ds(pl.multiple_of(owner * (PER_CORE * span) + j * span, span), span), :]

    for j in range(PER_CORE):
        probs, ml = score(j)
        half_ml[j] = ml
        half_num[j] = gather(j, probs).astype(jnp.bfloat16)
        if j == 0:
            for r in roots:
                @pl.when(plane == r)
                def _():
                    pl.semaphore_wait(barrier, len(targets) + 2 * len(guests[r]))

            @pl.when(jnp.logical_not(is_root))
            def _():
                pl.semaphore_wait(barrier, 1 + len(targets))
        for copy in to_partner(j):
            copy.start()

    for j in range(PER_CORE):
        probs, ml = score(PER_CORE + j)
        numer = gather(PER_CORE + j, probs)
        for copy in to_partner(j):
            copy.wait_recv()
        other = peer_ml[j]
        top = jnp.maximum(ml[0:1], other[0:1])
        mine = jnp.exp2((ml[0:1] - top) * SHIFT)
        theirs = jnp.exp2((other[0:1] - top) * SHIFT)
        chip_ml[j, chip] = jnp.concatenate([top, mine * ml[1:2] + theirs * other[1:2]], axis=0)
        columns = jnp.transpose(jnp.concatenate([mine, theirs, jnp.zeros((6, 128), jnp.float32)], axis=0))
        total = numer * columns[:block, 0:1] + peer_num[j].astype(jnp.float32) * columns[:block, 1:2]
        chip_num[j, chip] = total.astype(jnp.bfloat16)
        for i, target in enumerate(targets):
            @pl.when(chip != target)
            def _():
                for copy in to_root(j, i):
                    copy.start()

    @pl.when(is_root)
    def _():
        for j in range(PER_CORE):
            for k in range(1, chips):
                for copy in from_chip(j, k):
                    copy.wait_recv()
            maxima = [chip_ml[j, i][0:1] for i in range(chips)]
            top = functools.reduce(jnp.maximum, maxima)
            factors = [jnp.exp2((m - top) * SHIFT) for m in maxima]
            denom = sum(f * chip_ml[j, i][1:2] for i, f in enumerate(factors))
            factors = [f / denom for f in factors]
            pad = -chips % 8
            if pad:
                factors = factors + [jnp.zeros((pad, 128), jnp.float32)]
            columns = jnp.transpose(jnp.concatenate(factors, axis=0))
            numer = None
            for i in range(chips):
                term = chip_num[j, i].astype(jnp.float32) * columns[:block, i : i + 1]
                numer = term if numer is None else numer + term
            attended = numer.astype(jnp.bfloat16)
            for e in range(heads_each):
                for t in range(2):
                    base = pl.multiple_of(core * (PER_CORE * span) + j * span + e * tile, tile)
                    out[t, pl.ds(base, tile), :] = attended[e * rows + t * tile : e * rows + (t + 1) * tile]
            remote(part(core, j), part(core, j), ps.at[j], pr.at[j], partner).start()
            for r in roots:
                if guests[r]:
                    @pl.when(plane == r)
                    def _():
                        for i, guest in enumerate(guests[r]):
                            for d in range(2):
                                device = (guest * 2 + y) * 2 + d
                                remote(part(core, j), part(core, j), fs.at[j, i, d], fr.at[j, core], device).start()
        for j in range(PER_CORE):
            remote(part(core, j), part(1 - core, j), ps.at[j], pr.at[j], partner).wait_recv()
        for j in range(PER_CORE):
            remote(part(core, j), part(core, j), ps.at[j], pr.at[j], partner).wait_send()
            for r in roots:
                if guests[r]:
                    @pl.when(plane == r)
                    def _():
                        for i, guest in enumerate(guests[r]):
                            for d in range(2):
                                device = (guest * 2 + y) * 2 + d
                                remote(part(core, j), part(core, j), fs.at[j, i, d], fr.at[j, core], device).wait_send()

    @pl.when(jnp.logical_not(is_root))
    def _():
        for j in range(PER_CORE):
            for d in range(2):
                remote(part(d, j), part(d, j), fs.at[j, 0, d], fr.at[j, d], server * 2 + d).wait_recv()

    for j in range(PER_CORE):
        for copy in to_partner(j):
            copy.wait_send()
        for i, target in enumerate(targets):
            @pl.when(chip != target)
            def _():
                for copy in to_root(j, i):
                    copy.wait_send()


def per_device(n, queries, cache_k, cache_v, context_len, slot_seq, slot_pos):
    slots = cache_k.shape[0]
    seqs = queries.shape[1]
    heads = queries.shape[2] // HD
    rows = 2 * seqs * heads // KVH
    heads_each = KVH // CHUNKS
    block = heads_each * rows
    chips = n // 2
    fans = 2 * len(root_planes(chips // 2))
    vmem = pl.BlockSpec(memory_space=pltpu.VMEM)
    dma = pltpu.SemaphoreType.DMA
    anywhere = pl.BlockSpec(memory_space=pltpu.HBM)
    attended = pl.pallas_call(
        functools.partial(kernel, n),
        out_shape=jax.ShapeDtypeStruct((2, heads * seqs, HD), jnp.bfloat16),
        in_specs=[anywhere] * 6,
        out_specs=vmem,
        scratch_shapes=[
            pltpu.SMEM((seqs,), jnp.int32),
            pltpu.VMEM(queries.shape, jnp.bfloat16),
            pltpu.VMEM((1, slots), jnp.int32),
            pltpu.VMEM((1, slots), jnp.int32),
            pltpu.VMEM((CHUNKS, slots, heads_each * HD), jnp.bfloat16),
            pltpu.VMEM((CHUNKS, slots, heads_each * HD), jnp.bfloat16),
            pltpu.VMEM((KVH * rows, HD), jnp.float32),
            pltpu.VMEM((rows, slots), jnp.float32),
            pltpu.VMEM((PER_CORE, block, HD), jnp.bfloat16),
            pltpu.VMEM((PER_CORE, 2, 128), jnp.float32),
            pltpu.VMEM((PER_CORE, block, HD), jnp.bfloat16),
            pltpu.VMEM((PER_CORE, 2, 128), jnp.float32),
            pltpu.VMEM((PER_CORE, chips, block, HD), jnp.bfloat16),
            pltpu.VMEM((PER_CORE, chips, 2, 128), jnp.float32),
            dma((4,)), dma((CHUNKS,)), dma((CHUNKS,)),
            dma((PER_CORE,)), dma((PER_CORE,)), dma((PER_CORE,)), dma((PER_CORE,)),
            dma((PER_CORE, fans)), dma((PER_CORE, fans)), dma((PER_CORE, chips)), dma((PER_CORE, chips)),
            dma((PER_CORE,)), dma((PER_CORE,)),
            dma((PER_CORE, chips // 2, 2)), dma((PER_CORE, 2)),
        ],
        compiler_params=pltpu.CompilerParams(collective_id=0, has_side_effects=True, vmem_limit_bytes=LIMIT),
    )(*[
        pltpu.with_memory_space_constraint(x, pltpu.HBM)
        for x in (context_len, queries, cache_k, cache_v, slot_seq.reshape(1, slots), slot_pos.reshape(1, slots))
    ])
    steps = queries.shape[0]
    return attended.reshape(steps, heads, seqs, HD).transpose(0, 2, 1, 3).reshape(queries.shape)


def solution(mesh):
    return jax.shard_map(
        functools.partial(per_device, mesh.shape["seq"]),
        mesh=mesh,
        in_specs=(
            P(None, "parts", None),
            P(("parts", "seq"), None),
            P(("parts", "seq"), None),
            P("parts"),
            P(("parts", "seq")),
            P(("parts", "seq")),
        ),
        out_specs=P(None, "parts", None),
        check_vma=False,
    )
```

time: 18.4 us -> 16.7 us (0.908)
  Pallas kernels: 18.3 us -> 15.9 us
  local copies, waits for them, and re-layouts: 0 us -> 0.63 us
    pallas_call x1, Pallas kernels: 17.6 us -> 15.9 us  [per_device(): pl.pallas_call(functools.partial(kernel, n), out_shape=jax.ShapeDtypeStru...]
    pallas_call x1 -> x0, Pallas kernels: 0.71 us -> none  [per_device(): pl.pallas_call(place, out_shape=jax.ShapeDtypeStruct(queries.shape, jnp.b...]
    unnamed x0 -> x1, local copies, waits for them, and re-layouts: none -> 0.63 us
where the time goes in v1:
time: 16.7 us; the launch traced here: 16.6 us
  Pallas kernels  15.9 us (95%)
  local copies, waits for them, and re-layouts  0.63 us (4%)
    pallas_call x1, Pallas kernels, per_device(): pl.pallas_call(functools.partial(kernel, n), out_shape=jax.ShapeDtypeStru...  15.9 us
    unnamed x1, local copies, waits for them, and re-layouts  0.63 us

profile of v1, /device:TPU:0, one launch (start us, length us, event | category | flops | bytes accessed | tf_op | source)
XLA Modules:
  0.0 16.6 jit_solution(12913913271420420526)
XLA Ops:
  0.0 15.9 %shard_map.64 = bf16[2,128,128]{2,1,0:T(8,128)(2,1)S(1)} custom-call(s32[2]{0:T(128)} %ctx_hbm.1, bf16[2,2,8192]{2,1,0:T(2,128)(2,1)} %q_hbm.1, bf16[2048,1024]{1,0:T(8,128)(2,1)} %k_hbm.1, bf16[2048,1024]{1,0:T(8,128)(2,1)} %v_hbm.1, s32[1,2048]{1,0:T(1,128)} %bitcast.8, s32[1,2048]{1,0:T(1,128)} %bitcast.9), custom_call_target="tpu_custom_call" | custom-call | tf_op jit(solution)/shard_map/pallas_call | solution.py:287
  15.9 0.6 %copy.9 = bf16[2,2,8192]{2,1,0:T(2,128)(2,1)} copy(bf16[2,2,8192]{2,1,0:T(2,128)(2,1)S(1)} %bitcast.7) | data formatting | bytes 131072

commit v2 on v1

v2 whole, which is shorter than its diff:
```python
import functools

import jax
import jax.numpy as jnp
from jax import lax
from jax.experimental import pallas as pl
from jax.experimental.pallas import tpu as pltpu
from jax.sharding import PartitionSpec as P

KVH = 8
HD = 128
CHUNKS = 2
STEP = 256
LIMIT = 24 << 20
SHIFT = HD ** (-0.5) * 1.4426950408889634
HIDDEN = -1e30
MESH = pl.DeviceIdType.MESH


def served_by(plane, planes):
    return (planes // 2) * ((4 * plane // planes + 2) // 3)


def root_planes(planes):
    return (0, planes // 2) if planes > 1 else (0,)


def kernel(
    n, ctx_hbm, q_hbm, k_hbm, v_hbm, seq_hbm, pos_hbm, out,
    ctx, q_ref, seq_ref, pos_ref, kbuf, vbuf, qf, qt, bias, sbuf, pbuf,
    half_num, half_ml, peer_num, peer_ml, chip_num, chip_ml,
    isem, ksem, vsem, hs, hsm, hr, hrm, cs, csm, cr, crm, ps, pr, fs, fr,
):
    me = lax.axis_index("seq")
    chips = n // 2
    planes = chips // 2
    core = me % 2
    chip = me // 2
    y = chip % 2
    plane = chip // 2
    roots = root_planes(planes)
    is_root = functools.reduce(lambda a, b: a | b, [plane == r for r in roots])
    partner = chip * 2 + (1 - core)
    server = served_by(plane, planes) * 2 + y
    guests = {r: [p for p in range(planes) if p not in roots and served_by(p, planes) == r] for r in roots}
    halves = (1 - core, core)
    slots = k_hbm.shape[0]
    heads_half = KVH // 2
    heads_each = heads_half // CHUNKS
    wide = heads_half * HD
    width = heads_each * HD
    group = q_ref.shape[2] // HD // KVH
    seqs = q_ref.shape[1]
    rows = 2 * seqs * group
    lanes = heads_half * rows
    block = heads_each * rows
    tile = group * seqs
    span = heads_each * tile
    cut = slots // CHUNKS

    barrier = pltpu.get_barrier_semaphore()

    def greet(device):
        pl.semaphore_signal(barrier, inc=1, device_id={"seq": device}, device_id_type=MESH)

    inputs = []
    for i, (src, dst) in enumerate(((q_hbm, q_ref), (seq_hbm, seq_ref), (pos_hbm, pos_ref), (ctx_hbm, ctx))):
        copy = pltpu.make_async_copy(src, dst, isem.at[i])
        copy.start()
        inputs.append(copy)

    def first_column(order):
        half = core * order + (1 - core) * (1 - order)
        return half * wide

    def k_copy(i):
        order, part = i // CHUNKS, i % CHUNKS
        some = pl.ds(pl.multiple_of(part * cut, cut), cut)
        columns = pl.ds(pl.multiple_of(first_column(order), wide), wide)
        return pltpu.make_async_copy(k_hbm.at[some, columns], kbuf.at[order, some], ksem.at[i])

    def v_copy(i):
        order, part = i // CHUNKS, i % CHUNKS
        columns = pl.ds(pl.multiple_of(first_column(order) + part * width, width), width)
        return pltpu.make_async_copy(v_hbm.at[:, columns], vbuf.at[i], vsem.at[i])

    def load_k(i, carry):
        k_copy(i).start()
        return carry

    def load_v(i, carry):
        v_copy(i).start()
        return carry

    lax.fori_loop(0, 2 * CHUNKS, load_k, 0)
    lax.fori_loop(0, 2 * CHUNKS, load_v, 0)

    greet(partner)

    @pl.when(is_root)
    def _():
        for k in range(1, chips):
            greet((chip + k) % chips * 2 + core)

    @pl.when(jnp.logical_not(is_root))
    def _():
        for d in range(2):
            greet(server * 2 + d)

    for copy in inputs:
        copy.wait()

    for t in range(2):
        for head in range(KVH * group):
            g, h = head // group, head % group
            base = g * rows + t * group * seqs + h * seqs
            qf[base : base + seqs, :] = q_ref[t, :, head * HD : (head + 1) * HD].astype(jnp.float32)

    column = lax.broadcasted_iota(jnp.int32, (HD, lanes), 1)
    for order in range(2):
        turned = jnp.transpose(qf[pl.ds(pl.multiple_of(halves[order] * lanes, lanes), lanes), :])
        for e in range(heads_half):
            qt[order, e * HD : (e + 1) * HD, :] = jnp.where(column // rows == e, turned, 0.0).astype(jnp.bfloat16)

    masks = []
    for t in range(2):
        for sq in range(seqs):
            allowed = (seq_ref[...] == sq) & (pos_ref[...] <= ctx[sq] - 2 + t)
            masks.append(jnp.where(allowed, 0.0, HIDDEN))
    pad = -len(masks) % 16
    masks = jnp.concatenate(masks + [jnp.zeros((pad, slots), jnp.float32)], axis=0).astype(jnp.bfloat16)
    pick_row = lax.broadcasted_iota(jnp.int32, (2 * seqs + pad, lanes), 0)
    pick_lane = lax.broadcasted_iota(jnp.int32, (2 * seqs + pad, lanes), 1) % rows
    pick = (pick_lane // tile) * seqs + pick_lane % seqs == pick_row
    bias[...] = lax.dot_general(
        masks, jnp.where(pick, 1.0, 0.0).astype(jnp.bfloat16), (((0,), (0,)), ((), ())),
        preferred_element_type=jnp.float32,
    )

    def fold(x, op):
        return op(x.reshape(x.shape[0] // 8, 8, x.shape[1]), axis=0)

    def score(order, part, top):
        for b in range(part * cut, (part + 1) * cut, STEP):
            got = jnp.dot(
                kbuf[order, b : b + STEP, :], qt[order], preferred_element_type=jnp.float32
            ) + bias[b : b + STEP, :]
            sbuf[order, b : b + STEP, :] = got
            high = fold(got, jnp.max)
            top = high if top is None else jnp.maximum(top, high)
        return top

    def weigh(order, top):
        m = jnp.max(top, axis=0, keepdims=True)
        total = None
        for b in range(0, slots, STEP):
            w = jnp.exp2((sbuf[order, b : b + STEP, :] - m) * SHIFT)
            pbuf[order, b : b + STEP, :] = w.astype(jnp.bfloat16)
            part = fold(w, jnp.sum)
            total = part if total is None else total + part
        return jnp.concatenate([m, jnp.sum(total, axis=0, keepdims=True)], axis=0)

    def gather(order, j):
        full = lax.dot_general(
            pbuf[order], vbuf[order * CHUNKS + j], (((0,), (0,)), ((), ())), preferred_element_type=jnp.float32
        )
        return jnp.concatenate(
            [full[(j * heads_each + e) * rows : (j * heads_each + e + 1) * rows, e * HD : (e + 1) * HD] for e in range(heads_each)],
            axis=0,
        )

    def remote(src, dst, ss, rs, device):
        return pltpu.make_async_remote_copy(
            src_ref=src, dst_ref=dst, send_sem=ss, recv_sem=rs, device_id={"seq": device}, device_id_type=MESH
        )

    def ml_to_partner():
        return remote(half_ml, peer_ml, hsm, hrm, partner)

    def num_to_partner(j):
        return remote(half_num.at[j], peer_num.at[j], hs.at[j], hr.at[j], partner)

    targets = [r * 2 + side for r in roots for side in range(2)]

    def ml_to_root(i):
        return remote(chip_ml.at[chip], chip_ml.at[chip], csm.at[i], crm.at[chip], targets[i] * 2 + core)

    def num_to_root(j, i):
        return remote(chip_num.at[j, chip], chip_num.at[j, chip], cs.at[j, i], cr.at[j, chip], targets[i] * 2 + core)

    def ml_from_chip(k):
        slot = (chip + k) % chips
        return remote(chip_ml.at[slot], chip_ml.at[slot], csm.at[0], crm.at[slot], slot * 2 + core)

    def num_from_chip(j, k):
        slot = (chip + k) % chips
        return remote(chip_num.at[j, slot], chip_num.at[j, slot], cs.at[j, 0], cr.at[j, slot], slot * 2 + core)

    def part_of(owner, j):
        return out.at[:, pl.ds(pl.multiple_of(owner * (CHUNKS * span) + j * span, span), span), :]

    def elsewhere(i, act):
        @pl.when(chip != targets[i])
        def _():
            act()

    k_copy(0).wait()
    top = score(0, 0, None)
    k_copy(1).wait()
    top = score(0, 1, top)
    k_copy(2).wait()
    own_top = score(1, 0, None)
    half_ml[...] = weigh(0, top)
    k_copy(3).wait()
    own_top = score(1, 1, own_top)
    for r in roots:
        @pl.when(plane == r)
        def _():
            pl.semaphore_wait(barrier, len(targets) + 2 * len(guests[r]))

    @pl.when(jnp.logical_not(is_root))
    def _():
        pl.semaphore_wait(barrier, 1 + len(targets))

    ml_to_partner().start()
    for j in range(CHUNKS):
        v_copy(j).wait()
    ml = weigh(1, own_top)
    for j in range(CHUNKS):
        half_num[j] = gather(0, j).astype(jnp.bfloat16)
        num_to_partner(j).start()

    v_copy(CHUNKS).wait()
    numers = [gather(1, 0)]
    ml_to_partner().wait_recv()
    other = peer_ml[...]
    top = jnp.maximum(ml[0:1], other[0:1])
    mine = jnp.exp2((ml[0:1] - top) * SHIFT)
    theirs = jnp.exp2((other[0:1] - top) * SHIFT)
    chip_ml[chip] = jnp.concatenate([top, mine * ml[1:2] + theirs * other[1:2]], axis=0)
    columns = jnp.transpose(jnp.concatenate([mine, theirs, jnp.zeros((6, lanes), jnp.float32)], axis=0))
    for i in range(len(targets)):
        elsewhere(i, lambda: ml_to_root(i).start())
    for j in range(1, CHUNKS):
        v_copy(CHUNKS + j).wait()
        numers.append(gather(1, j))
    for j in range(CHUNKS):
        num_to_partner(j).wait_recv()
        some = slice(j * block, (j + 1) * block)
        total = numers[j] * columns[some, 0:1] + peer_num[j].astype(jnp.float32) * columns[some, 1:2]
        chip_num[j, chip] = total.astype(jnp.bfloat16)
        for i in range(2):
            elsewhere(i, lambda: num_to_root(j, i).start())
    for j in range(CHUNKS):
        for i in range(2, len(targets)):
            elsewhere(i, lambda: num_to_root(j, i).start())

    @pl.when(is_root)
    def _():
        for k in range(1, chips):
            ml_from_chip(k).wait_recv()
        maxima = [chip_ml[i][0:1] for i in range(chips)]
        top = functools.reduce(jnp.maximum, maxima)
        factors = [jnp.exp2((m - top) * SHIFT) for m in maxima]
        denom = sum(f * chip_ml[i][1:2] for i, f in enumerate(factors))
        factors = [f / denom for f in factors]
        pad = -chips % 8
        if pad:
            factors = factors + [jnp.zeros((pad, lanes), jnp.float32)]
        columns = jnp.transpose(jnp.concatenate(factors, axis=0))
        for j in range(CHUNKS):
            for k in range(1, chips):
                num_from_chip(j, k).wait_recv()
            numer = None
            for i in range(chips):
                term = chip_num[j, i].astype(jnp.float32) * columns[j * block : (j + 1) * block, i : i + 1]
                numer = term if numer is None else numer + term
            attended = numer.astype(jnp.bfloat16)
            for e in range(heads_each):
                for t in range(2):
                    base = pl.multiple_of(core * (CHUNKS * span) + j * span + e * tile, tile)
                    out[t, pl.ds(base, tile), :] = attended[e * rows + t * tile : e * rows + (t + 1) * tile]
            remote(part_of(core, j), part_of(core, j), ps.at[j], pr.at[j], partner).start()
            for r in roots:
                if guests[r]:
                    @pl.when(plane == r)
                    def _():
                        for i, guest in enumerate(guests[r]):
                            for d in range(2):
                                device = (guest * 2 + y) * 2 + d
                                remote(part_of(core, j), part_of(core, j), fs.at[j, i, d], fr.at[j, core], device).start()
        for j in range(CHUNKS):
            remote(part_of(core, j), part_of(1 - core, j), ps.at[j], pr.at[j], partner).wait_recv()
        for j in range(CHUNKS):
            remote(part_of(core, j), part_of(core, j), ps.at[j], pr.at[j], partner).wait_send()
            for r in roots:
                if guests[r]:
                    @pl.when(plane == r)
                    def _():
                        for i, guest in enumerate(guests[r]):
                            for d in range(2):
                                device = (guest * 2 + y) * 2 + d
                                remote(part_of(core, j), part_of(core, j), fs.at[j, i, d], fr.at[j, core], device).wait_send()

    @pl.when(jnp.logical_not(is_root))
    def _():
        for j in range(CHUNKS):
            for d in range(2):
                remote(part_of(d, j), part_of(d, j), fs.at[j, 0, d], fr.at[j, d], server * 2 + d).wait_recv()

    ml_to_partner().wait_send()
    for j in range(CHUNKS):
        num_to_partner(j).wait_send()
    for i in range(len(targets)):
        elsewhere(i, lambda: ml_to_root(i).wait_send())
        for j in range(CHUNKS):
            elsewhere(i, lambda: num_to_root(j, i).wait_send())


def per_device(n, queries, cache_k, cache_v, context_len, slot_seq, slot_pos):
    slots = cache_k.shape[0]
    seqs = queries.shape[1]
    heads = queries.shape[2] // HD
    rows = 2 * seqs * heads // KVH
    heads_half = KVH // 2
    lanes = heads_half * rows
    block = lanes // CHUNKS
    chips = n // 2
    fans = 2 * len(root_planes(chips // 2))
    vmem = pl.BlockSpec(memory_space=pltpu.VMEM)
    dma = pltpu.SemaphoreType.DMA
    anywhere = pl.BlockSpec(memory_space=pltpu.HBM)
    attended = pl.pallas_call(
        functools.partial(kernel, n),
        out_shape=jax.ShapeDtypeStruct((2, heads * seqs, HD), jnp.bfloat16),
        in_specs=[anywhere] * 6,
        out_specs=vmem,
        scratch_shapes=[
            pltpu.SMEM((seqs,), jnp.int32),
            pltpu.VMEM(queries.shape, jnp.bfloat16),
            pltpu.VMEM((1, slots), jnp.int32),
            pltpu.VMEM((1, slots), jnp.int32),
            pltpu.VMEM((2, slots, heads_half * HD), jnp.bfloat16),
            pltpu.VMEM((2 * CHUNKS, slots, heads_half * HD // CHUNKS), jnp.bfloat16),
            pltpu.VMEM((KVH * rows, HD), jnp.float32),
            pltpu.VMEM((2, heads_half * HD, lanes), jnp.bfloat16),
            pltpu.VMEM((slots, lanes), jnp.float32),
            pltpu.VMEM((2, slots, lanes), jnp.float32),
            pltpu.VMEM((2, slots, lanes), jnp.bfloat16),
            pltpu.VMEM((CHUNKS, block, HD), jnp.bfloat16),
            pltpu.VMEM((2, lanes), jnp.float32),
            pltpu.VMEM((CHUNKS, block, HD), jnp.bfloat16),
            pltpu.VMEM((2, lanes), jnp.float32),
            pltpu.VMEM((CHUNKS, chips, block, HD), jnp.bfloat16),
            pltpu.VMEM((chips, 2, lanes), jnp.float32),
            dma((4,)), dma((2 * CHUNKS,)), dma((2 * CHUNKS,)),
            dma((CHUNKS,)), dma(()), dma((CHUNKS,)), dma(()),
            dma((CHUNKS, fans)), dma((fans,)), dma((CHUNKS, chips)), dma((chips,)),
            dma((CHUNKS,)), dma((CHUNKS,)),
            dma((CHUNKS, chips // 2, 2)), dma((CHUNKS, 2)),
        ],
        compiler_params=pltpu.CompilerParams(collective_id=0, has_side_effects=True, vmem_limit_bytes=LIMIT),
    )(*[
        pltpu.with_memory_space_constraint(x, pltpu.HBM)
        for x in (context_len, queries, cache_k, cache_v, slot_seq.reshape(1, slots), slot_pos.reshape(1, slots))
    ])
    steps = queries.shape[0]
    return attended.reshape(steps, heads, seqs, HD).transpose(0, 2, 1, 3).reshape(queries.shape)


def solution(mesh):
    return jax.shard_map(
        functools.partial(per_device, mesh.shape["seq"]),
        mesh=mesh,
        in_specs=(
            P(None, "parts", None),
            P(("parts", "seq"), None),
            P(("parts", "seq"), None),
            P("parts"),
            P(("parts", "seq")),
            P(("parts", "seq")),
        ),
        out_specs=P(None, "parts", None),
        check_vma=False,
    )
```

time: 16.7 us -> 16.7 us (level)
  no operation moved by 1% of the time
where the time goes in v2:
time: 16.7 us; the launch traced here: 16.6 us
  Pallas kernels  15.9 us (95%)
  local copies, waits for them, and re-layouts  0.63 us (4%)
    pallas_call x1, Pallas kernels, per_device(): pl.pallas_call(functools.partial(kernel, n), out_shape=jax.ShapeDtypeStru...  15.9 us
    unnamed x1, local copies, waits for them, and re-layouts  0.63 us

profile of v2, /device:TPU:0, one launch (start us, length us, event | category | flops | bytes accessed | tf_op | source)
XLA Modules:
  0.0 16.6 jit_solution(10011361872881963437)
XLA Ops:
  0.0 15.9 %shard_map.64 = bf16[2,128,128]{2,1,0:T(8,128)(2,1)S(1)} custom-call(s32[2]{0:T(128)} %ctx_hbm.1, bf16[2,2,8192]{2,1,0:T(2,128)(2,1)} %q_hbm.1, bf16[2048,1024]{1,0:T(8,128)(2,1)} %k_hbm.1, bf16[2048,1024]{1,0:T(8,128)(2,1)} %v_hbm.1, s32[1,2048]{1,0:T(1,128)} %bitcast.8, s32[1,2048]{1,0:T(1,128)} %bitcast.9), custom_call_target="tpu_custom_call" | custom-call | tf_op jit(solution)/shard_map/pallas_call | solution.py:333
  16.0 0.6 %copy.9 = bf16[2,2,8192]{2,1,0:T(2,128)(2,1)} copy(bf16[2,2,8192]{2,1,0:T(2,128)(2,1)S(1)} %bitcast.7) | data formatting | bytes 131072

commit v3 on v2

--- a/solution.py
+++ b/solution.py
@@ -208,11 +208,12 @@
     top = score(0, 0, None)
     k_copy(1).wait()
     top = score(0, 1, top)
-    k_copy(2).wait()
-    own_top = score(1, 0, None)
+    for i in range(CHUNKS, 2 * CHUNKS):
+        k_copy(i).wait()
     half_ml[...] = weigh(0, top)
-    k_copy(3).wait()
-    own_top = score(1, 1, own_top)
+    own_top = None
+    for part in range(CHUNKS):
+        own_top = score(1, part, own_top)
     for r in roots:
         @pl.when(plane == r)
         def _():
@@ -230,8 +231,9 @@
         half_num[j] = gather(0, j).astype(jnp.bfloat16)
         num_to_partner(j).start()
 
-    v_copy(CHUNKS).wait()
-    numers = [gather(1, 0)]
+    for j in range(CHUNKS):
+        v_copy(CHUNKS + j).wait()
+    numers = [gather(1, j) for j in range(CHUNKS)]
     ml_to_partner().wait_recv()
     other = peer_ml[...]
     top = jnp.maximum(ml[0:1], other[0:1])
@@ -241,18 +243,19 @@
     columns = jnp.transpose(jnp.concatenate([mine, theirs, jnp.zeros((6, lanes), jnp.float32)], axis=0))
     for i in range(len(targets)):
         elsewhere(i, lambda: ml_to_root(i).start())
-    for j in range(1, CHUNKS):
-        v_copy(CHUNKS + j).wait()
-        numers.append(gather(1, j))
     for j in range(CHUNKS):
         num_to_partner(j).wait_recv()
         some = slice(j * block, (j + 1) * block)
         total = numers[j] * columns[some, 0:1] + peer_num[j].astype(jnp.float32) * columns[some, 1:2]
         chip_num[j, chip] = total.astype(jnp.bfloat16)
-        for i in range(2):
-            elsewhere(i, lambda: num_to_root(j, i).start())
-    for j in range(CHUNKS):
-        for i in range(2, len(targets)):
+        elsewhere(0, lambda: num_to_root(j, 0).start())
+    @pl.when(core == 1)
+    def _():
+        for j in range(CHUNKS):
+            elsewhere(0, lambda: num_to_root(j, 0).wait_send())
+
+    for i in (2, 3, 1):
+        for j in range(CHUNKS):
             elsewhere(i, lambda: num_to_root(j, i).start())
 
     @pl.when(is_root)
@@ -314,7 +317,12 @@
     for i in range(len(targets)):
         elsewhere(i, lambda: ml_to_root(i).wait_send())
         for j in range(CHUNKS):
-            elsewhere(i, lambda: num_to_root(j, i).wait_send())
+            if i:
+                elsewhere(i, lambda: num_to_root(j, i).wait_send())
+            else:
+                @pl.when(core == 0)
+                def _():
+                    elsewhere(0, lambda: num_to_root(j, 0).wait_send())
 
 
 def per_device(n, queries, cache_k, cache_v, context_len, slot_seq, slot_pos):

time: 16.7 us -> 15.7 us (0.940)
  the two profiles are of different devices: /device:TPU:0 before, /device:TPU:11 now
where the time goes in v3:
time: 15.7 us; the launch traced here: 15.5 us
  Pallas kernels  14.9 us (95%)
  local copies, waits for them, and re-layouts  0.63 us (4%)
    pallas_call x1, Pallas kernels, per_device(): pl.pallas_call(functools.partial(kernel, n), out_shape=jax.ShapeDtypeStru...  14.9 us
    unnamed x1, local copies, waits for them, and re-layouts  0.63 us

profile of v3, /device:TPU:11, one launch (start us, length us, event | category | flops | bytes accessed | tf_op | source)
XLA Modules:
  0.0 15.5 jit_solution(6741157164207846511)
XLA Ops:
  0.0 14.9 %shard_map.64 = bf16[2,128,128]{2,1,0:T(8,128)(2,1)S(1)} custom-call(s32[2]{0:T(128)} %ctx_hbm.1, bf16[2,2,8192]{2,1,0:T(2,128)(2,1)} %q_hbm.1, bf16[2048,1024]{1,0:T(8,128)(2,1)} %k_hbm.1, bf16[2048,1024]{1,0:T(8,128)(2,1)} %v_hbm.1, s32[1,2048]{1,0:T(1,128)} %bitcast.8, s32[1,2048]{1,0:T(1,128)} %bitcast.9), custom_call_target="tpu_custom_call" | custom-call | tf_op jit(solution)/shard_map/pallas_call | solution.py:341
  14.9 0.6 %copy.9 = bf16[2,2,8192]{2,1,0:T(2,128)(2,1)} copy(bf16[2,2,8192]{2,1,0:T(2,128)(2,1)S(1)} %bitcast.7) | data formatting | bytes 131072

commit v4 on v3

--- a/solution.py
+++ b/solution.py
@@ -92,8 +92,10 @@
         v_copy(i).start()
         return carry
 
-    lax.fori_loop(0, 2 * CHUNKS, load_k, 0)
-    lax.fori_loop(0, 2 * CHUNKS, load_v, 0)
+    lax.fori_loop(0, 3, load_k, 0)
+    lax.fori_loop(0, 2, load_v, 0)
+    k_copy(3).start()
+    lax.fori_loop(2, 4, load_v, 0)
 
     greet(partner)
 
@@ -208,12 +210,9 @@
     top = score(0, 0, None)
     k_copy(1).wait()
     top = score(0, 1, top)
-    for i in range(CHUNKS, 2 * CHUNKS):
-        k_copy(i).wait()
+    k_copy(2).wait()
     half_ml[...] = weigh(0, top)
-    own_top = None
-    for part in range(CHUNKS):
-        own_top = score(1, part, own_top)
+    own_top = score(1, 0, None)
     for r in roots:
         @pl.when(plane == r)
         def _():
@@ -226,14 +225,13 @@
     ml_to_partner().start()
     for j in range(CHUNKS):
         v_copy(j).wait()
+    for j in range(CHUNKS):
+        half_num[j] = gather(0, j).astype(jnp.bfloat16)
+    for j in range(CHUNKS):
+        num_to_partner(j).start()
+    k_copy(3).wait()
+    own_top = score(1, 1, own_top)
     ml = weigh(1, own_top)
-    for j in range(CHUNKS):
-        half_num[j] = gather(0, j).astype(jnp.bfloat16)
-        num_to_partner(j).start()
-
-    for j in range(CHUNKS):
-        v_copy(CHUNKS + j).wait()
-    numers = [gather(1, j) for j in range(CHUNKS)]
     ml_to_partner().wait_recv()
     other = peer_ml[...]
     top = jnp.maximum(ml[0:1], other[0:1])
@@ -243,6 +241,9 @@
     columns = jnp.transpose(jnp.concatenate([mine, theirs, jnp.zeros((6, lanes), jnp.float32)], axis=0))
     for i in range(len(targets)):
         elsewhere(i, lambda: ml_to_root(i).start())
+    for j in range(CHUNKS):
+        v_copy(CHUNKS + j).wait()
+    numers = [gather(1, j) for j in range(CHUNKS)]
     for j in range(CHUNKS):
         num_to_partner(j).wait_recv()
         some = slice(j * block, (j + 1) * block)

time: 15.7 us -> 15.5 us (0.987)
  Pallas kernels: 14.9 us -> 14.7 us
    pallas_call x1, Pallas kernels: 14.9 us -> 14.7 us  [per_device(): pl.pallas_call(functools.partial(kernel, n), out_shape=jax.ShapeDtypeStru...]
where the time goes in v4:
time: 15.5 us; the launch traced here: 15.4 us
  Pallas kernels  14.7 us (95%)
  local copies, waits for them, and re-layouts  0.63 us (4%)
    pallas_call x1, Pallas kernels, per_device(): pl.pallas_call(functools.partial(kernel, n), out_shape=jax.ShapeDtypeStru...  14.7 us
    unnamed x1, local copies, waits for them, and re-layouts  0.63 us

profile of v4, /device:TPU:11, one launch (start us, length us, event | category | flops | bytes accessed | tf_op | source)
XLA Modules:
  0.0 15.4 jit_solution(3633136510713205622)
XLA Ops:
  0.0 14.7 %shard_map.64 = bf16[2,128,128]{2,1,0:T(8,128)(2,1)S(1)} custom-call(s32[2]{0:T(128)} %ctx_hbm.1, bf16[2,2,8192]{2,1,0:T(2,128)(2,1)} %q_hbm.1, bf16[2048,1024]{1,0:T(8,128)(2,1)} %k_hbm.1, bf16[2048,1024]{1,0:T(8,128)(2,1)} %v_hbm.1, s32[1,2048]{1,0:T(1,128)} %bitcast.8, s32[1,2048]{1,0:T(1,128)} %bitcast.9), custom_call_target="tpu_custom_call" | custom-call | tf_op jit(solution)/shard_map/pallas_call | solution.py:342
  14.7 0.6 %copy.9 = bf16[2,2,8192]{2,1,0:T(2,128)(2,1)} copy(bf16[2,2,8192]{2,1,0:T(2,128)(2,1)S(1)} %bitcast.7) | data formatting | bytes 131072

commit v5 on v4

--- a/solution.py
+++ b/solution.py
@@ -15,14 +15,6 @@
 SHIFT = HD ** (-0.5) * 1.4426950408889634
 HIDDEN = -1e30
 MESH = pl.DeviceIdType.MESH
-
-
-def served_by(plane, planes):
-    return (planes // 2) * ((4 * plane // planes + 2) // 3)
-
-
-def root_planes(planes):
-    return (0, planes // 2) if planes > 1 else (0,)
 
 
 def kernel(
@@ -38,11 +30,12 @@
     chip = me // 2
     y = chip % 2
     plane = chip // 2
-    roots = root_planes(planes)
-    is_root = functools.reduce(lambda a, b: a | b, [plane == r for r in roots])
+    middle = planes // 2
+    first, central = plane == 0, plane == middle
+    guests = [p for p in range(planes) if p not in (0, middle)]
+    guest = jnp.logical_not(first | central)
     partner = chip * 2 + (1 - core)
-    server = served_by(plane, planes) * 2 + y
-    guests = {r: [p for p in range(planes) if p not in roots and served_by(p, planes) == r] for r in roots}
+    across = (plane * 2 + (1 - y)) * 2
     halves = (1 - core, core)
     slots = k_hbm.shape[0]
     heads_half = KVH // 2
@@ -99,15 +92,19 @@
 
     greet(partner)
 
-    @pl.when(is_root)
+    @pl.when(first | central)
     def _():
         for k in range(1, chips):
             greet((chip + k) % chips * 2 + core)
 
-    @pl.when(jnp.logical_not(is_root))
-    def _():
-        for d in range(2):
-            greet(server * 2 + d)
+    @pl.when(central)
+    def _():
+        greet(across + (1 - core))
+
+    @pl.when(guest)
+    def _():
+        for d in range(4):
+            greet(middle * 4 + d)
 
     for copy in inputs:
         copy.wait()
@@ -157,17 +154,20 @@
         total = None
         for b in range(0, slots, STEP):
             w = jnp.exp2((sbuf[order, b : b + STEP, :] - m) * SHIFT)
-            pbuf[order, b : b + STEP, :] = w.astype(jnp.bfloat16)
+            pbuf[order, :, b : b + STEP] = jnp.transpose(w.astype(jnp.bfloat16))
             part = fold(w, jnp.sum)
             total = part if total is None else total + part
         return jnp.concatenate([m, jnp.sum(total, axis=0, keepdims=True)], axis=0)
 
     def gather(order, j):
-        full = lax.dot_general(
-            pbuf[order], vbuf[order * CHUNKS + j], (((0,), (0,)), ((), ())), preferred_element_type=jnp.float32
-        )
         return jnp.concatenate(
-            [full[(j * heads_each + e) * rows : (j * heads_each + e + 1) * rows, e * HD : (e + 1) * HD] for e in range(heads_each)],
+            [
+                jnp.dot(
+                    pbuf[order, (j * heads_each + e) * rows : (j * heads_each + e + 1) * rows, :],
+                    vbuf[order * CHUNKS + j, :, e * HD : (e + 1) * HD], preferred_element_type=jnp.float32,
+                )
+                for e in range(heads_each)
+            ],
             axis=0,
         )
 
@@ -182,7 +182,7 @@
     def num_to_partner(j):
         return remote(half_num.at[j], peer_num.at[j], hs.at[j], hr.at[j], partner)
 
-    targets = [r * 2 + side for r in roots for side in range(2)]
+    targets = [0, 1, middle * 2, middle * 2 + 1]
 
     def ml_to_root(i):
         return remote(chip_ml.at[chip], chip_ml.at[chip], csm.at[i], crm.at[chip], targets[i] * 2 + core)
@@ -213,14 +213,17 @@
     k_copy(2).wait()
     half_ml[...] = weigh(0, top)
     own_top = score(1, 0, None)
-    for r in roots:
-        @pl.when(plane == r)
-        def _():
-            pl.semaphore_wait(barrier, len(targets) + 2 * len(guests[r]))
-
-    @pl.when(jnp.logical_not(is_root))
-    def _():
-        pl.semaphore_wait(barrier, 1 + len(targets))
+    @pl.when(first)
+    def _():
+        pl.semaphore_wait(barrier, 4)
+
+    @pl.when(central)
+    def _():
+        pl.semaphore_wait(barrier, 5 + 4 * len(guests))
+
+    @pl.when(guest)
+    def _():
+        pl.semaphore_wait(barrier, 5)
 
     ml_to_partner().start()
     for j in range(CHUNKS):
@@ -250,17 +253,40 @@
         total = numers[j] * columns[some, 0:1] + peer_num[j].astype(jnp.float32) * columns[some, 1:2]
         chip_num[j, chip] = total.astype(jnp.bfloat16)
         elsewhere(0, lambda: num_to_root(j, 0).start())
+    for j in range(CHUNKS):
+        elsewhere(2 + j, lambda: num_to_root(j, 2 + j).start())
     @pl.when(core == 1)
     def _():
         for j in range(CHUNKS):
             elsewhere(0, lambda: num_to_root(j, 0).wait_send())
 
-    for i in (2, 3, 1):
-        for j in range(CHUNKS):
-            elsewhere(i, lambda: num_to_root(j, i).start())
-
-    @pl.when(is_root)
-    def _():
+    for j in range(CHUNKS):
+        elsewhere(1, lambda: num_to_root(j, 1).start())
+
+    def share(j):
+        yield (0, partner), remote(part_of(core, j), part_of(core, j), fs.at[0], fr.at[core, j], partner)
+        for d in range(2):
+            yield (1 + d, across + d), remote(part_of(core, j), part_of(core, j), fs.at[1 + d], fr.at[core, j], across + d)
+        for g, p in enumerate(guests):
+            for d in range(4):
+                yield (3 + 4 * g + d, p * 4 + d), remote(
+                    part_of(core, j), part_of(core, j), fs.at[3 + 4 * g + d], fr.at[core, j], p * 4 + d
+                )
+
+    def collect(j, columns):
+        for k in range(1, chips):
+            num_from_chip(j, k).wait_recv()
+        numer = None
+        for i in range(chips):
+            term = chip_num[j, i].astype(jnp.float32) * columns[j * block : (j + 1) * block, i : i + 1]
+            numer = term if numer is None else numer + term
+        attended = numer.astype(jnp.bfloat16)
+        for e in range(heads_each):
+            for t in range(2):
+                base = pl.multiple_of(core * (CHUNKS * span) + j * span + e * tile, tile)
+                out[t, pl.ds(base, tile), :] = attended[e * rows + t * tile : e * rows + (t + 1) * tile]
+
+    def factors_of_chips():
         for k in range(1, chips):
             ml_from_chip(k).wait_recv()
         maxima = [chip_ml[i][0:1] for i in range(chips)]
@@ -271,59 +297,52 @@
         pad = -chips % 8
         if pad:
             factors = factors + [jnp.zeros((pad, lanes), jnp.float32)]
-        columns = jnp.transpose(jnp.concatenate(factors, axis=0))
+        return jnp.transpose(jnp.concatenate(factors, axis=0))
+
+    def swap(j, owner):
+        return remote(part_of(core, j), part_of(owner, j), ps.at[j], pr.at[j], partner)
+
+    @pl.when(first)
+    def _():
+        columns = factors_of_chips()
         for j in range(CHUNKS):
-            for k in range(1, chips):
-                num_from_chip(j, k).wait_recv()
-            numer = None
-            for i in range(chips):
-                term = chip_num[j, i].astype(jnp.float32) * columns[j * block : (j + 1) * block, i : i + 1]
-                numer = term if numer is None else numer + term
-            attended = numer.astype(jnp.bfloat16)
-            for e in range(heads_each):
-                for t in range(2):
-                    base = pl.multiple_of(core * (CHUNKS * span) + j * span + e * tile, tile)
-                    out[t, pl.ds(base, tile), :] = attended[e * rows + t * tile : e * rows + (t + 1) * tile]
-            remote(part_of(core, j), part_of(core, j), ps.at[j], pr.at[j], partner).start()
-            for r in roots:
-                if guests[r]:
-                    @pl.when(plane == r)
-                    def _():
-                        for i, guest in enumerate(guests[r]):
-                            for d in range(2):
-                                device = (guest * 2 + y) * 2 + d
-                                remote(part_of(core, j), part_of(core, j), fs.at[j, i, d], fr.at[j, core], device).start()
+            collect(j, columns)
+            swap(j, core).start()
         for j in range(CHUNKS):
-            remote(part_of(core, j), part_of(1 - core, j), ps.at[j], pr.at[j], partner).wait_recv()
+            swap(j, 1 - core).wait_recv()
         for j in range(CHUNKS):
-            remote(part_of(core, j), part_of(core, j), ps.at[j], pr.at[j], partner).wait_send()
-            for r in roots:
-                if guests[r]:
-                    @pl.when(plane == r)
-                    def _():
-                        for i, guest in enumerate(guests[r]):
-                            for d in range(2):
-                                device = (guest * 2 + y) * 2 + d
-                                remote(part_of(core, j), part_of(core, j), fs.at[j, i, d], fr.at[j, core], device).wait_send()
-
-    @pl.when(jnp.logical_not(is_root))
-    def _():
-        for j in range(CHUNKS):
-            for d in range(2):
-                remote(part_of(d, j), part_of(d, j), fs.at[j, 0, d], fr.at[j, d], server * 2 + d).wait_recv()
+            swap(j, core).wait_send()
+
+    for j in range(CHUNKS):
+        @pl.when(central & (y == j))
+        def _():
+            collect(j, factors_of_chips())
+            for _, copy in share(j):
+                copy.start()
+
+    @pl.when(jnp.logical_not(first))
+    def _():
+        for d in range(2):
+            for j in range(CHUNKS):
+                @pl.when(jnp.logical_not(central & (core == d) & (y == j)))
+                def _():
+                    remote(part_of(d, j), part_of(d, j), fs.at[0], fr.at[d, j], (middle * 2 + j) * 2 + d).wait_recv()
+
+    for j in range(CHUNKS):
+        @pl.when(central & (y == j))
+        def _():
+            for _, copy in share(j):
+                copy.wait_send()
 
     ml_to_partner().wait_send()
     for j in range(CHUNKS):
         num_to_partner(j).wait_send()
+        for i in (0, 1, 2 + j):
+            @pl.when((core == 0) | (i != 0))
+            def _():
+                elsewhere(i, lambda: num_to_root(j, i).wait_send())
     for i in range(len(targets)):
         elsewhere(i, lambda: ml_to_root(i).wait_send())
-        for j in range(CHUNKS):
-            if i:
-                elsewhere(i, lambda: num_to_root(j, i).wait_send())
-            else:
-                @pl.when(core == 0)
-                def _():
-                    elsewhere(0, lambda: num_to_root(j, 0).wait_send())
 
 
 def per_device(n, queries, cache_k, cache_v, context_len, slot_seq, slot_pos):
@@ -335,7 +354,6 @@
     lanes = heads_half * rows
     block = lanes // CHUNKS
     chips = n // 2
-    fans = 2 * len(root_planes(chips // 2))
     vmem = pl.BlockSpec(memory_space=pltpu.VMEM)
     dma = pltpu.SemaphoreType.DMA
     anywhere = pl.BlockSpec(memory_space=pltpu.HBM)
@@ -355,7 +373,7 @@
             pltpu.VMEM((2, heads_half * HD, lanes), jnp.bfloat16),
             pltpu.VMEM((slots, lanes), jnp.float32),
             pltpu.VMEM((2, slots, lanes), jnp.float32),
-            pltpu.VMEM((2, slots, lanes), jnp.bfloat16),
+            pltpu.VMEM((2, lanes, slots), jnp.bfloat16),
             pltpu.VMEM((CHUNKS, block, HD), jnp.bfloat16),
             pltpu.VMEM((2, lanes), jnp.float32),
             pltpu.VMEM((CHUNKS, block, HD), jnp.bfloat16),
@@ -364,9 +382,9 @@
             pltpu.VMEM((chips, 2, lanes), jnp.float32),
             dma((4,)), dma((2 * CHUNKS,)), dma((2 * CHUNKS,)),
             dma((CHUNKS,)), dma(()), dma((CHUNKS,)), dma(()),
-            dma((CHUNKS, fans)), dma((fans,)), dma((CHUNKS, chips)), dma((chips,)),
+            dma((CHUNKS, 4)), dma((4,)), dma((CHUNKS, chips)), dma((chips,)),
             dma((CHUNKS,)), dma((CHUNKS,)),
-            dma((CHUNKS, chips // 2, 2)), dma((CHUNKS, 2)),
+            dma((4 * chips,)), dma((2, CHUNKS)),
         ],
         compiler_params=pltpu.CompilerParams(collective_id=0, has_side_effects=True, vmem_limit_bytes=LIMIT),
     )(*[

time: 15.5 us -> 15.2 us (0.981)
  the two profiles are of different devices: /device:TPU:11 before, /device:TPU:0 now
where the time goes in v5:
time: 15.2 us; the launch traced here: 15.1 us
  Pallas kernels  14.4 us (95%)
  local copies, waits for them, and re-layouts  0.63 us (4%)
    pallas_call x1, Pallas kernels, per_device(): pl.pallas_call(functools.partial(kernel, n), out_shape=jax.ShapeDtypeStru...  14.4 us
    unnamed x1, local copies, waits for them, and re-layouts  0.63 us

profile of v5, /device:TPU:0, one launch (start us, length us, event | category | flops | bytes accessed | tf_op | source)
XLA Modules:
  0.0 15.1 jit_solution(16548537374298055299)
XLA Ops:
  0.0 14.4 %shard_map.64 = bf16[2,128,128]{2,1,0:T(8,128)(2,1)S(1)} custom-call(s32[2]{0:T(128)} %ctx_hbm.1, bf16[2,2,8192]{2,1,0:T(2,128)(2,1)} %q_hbm.1, bf16[2048,1024]{1,0:T(8,128)(2,1)} %k_hbm.1, bf16[2048,1024]{1,0:T(8,128)(2,1)} %v_hbm.1, s32[1,2048]{1,0:T(1,128)} %bitcast.8, s32[1,2048]{1,0:T(1,128)} %bitcast.9), custom_call_target="tpu_custom_call" | custom-call | tf_op jit(solution)/shard_map/pallas_call | solution.py:360
  14.4 0.6 %copy.9 = bf16[2,2,8192]{2,1,0:T(2,128)(2,1)} copy(bf16[2,2,8192]{2,1,0:T(2,128)(2,1)S(1)} %bitcast.7) | data formatting | bytes 131072

commit v6 on v5

--- a/solution.py
+++ b/solution.py
@@ -21,7 +21,7 @@
     n, ctx_hbm, q_hbm, k_hbm, v_hbm, seq_hbm, pos_hbm, out,
     ctx, q_ref, seq_ref, pos_ref, kbuf, vbuf, qf, qt, bias, sbuf, pbuf,
     half_num, half_ml, peer_num, peer_ml, chip_num, chip_ml,
-    isem, ksem, vsem, hs, hsm, hr, hrm, cs, csm, cr, crm, ps, pr, fs, fr,
+    isem, ksem, vsem, peer_sem, ml_sem, num_sem, fin,
 ):
     me = lax.axis_index("seq")
     chips = n // 2
@@ -75,7 +75,7 @@
     def v_copy(i):
         order, part = i // CHUNKS, i % CHUNKS
         columns = pl.ds(pl.multiple_of(first_column(order) + part * width, width), width)
-        return pltpu.make_async_copy(v_hbm.at[:, columns], vbuf.at[i], vsem.at[i])
+        return pltpu.make_async_copy(v_hbm.at[:, columns], vbuf.at[i], vsem.at[order])
 
     def load_k(i, carry):
         k_copy(i).start()
@@ -171,32 +171,30 @@
             axis=0,
         )
 
+    def drain(ref, sem):
+        pltpu.make_async_copy(ref, ref, sem).wait()
+
+    rest_sent, ml_sent, first_sent, shared = (isem.at[i] for i in range(4))
+
     def remote(src, dst, ss, rs, device):
         return pltpu.make_async_remote_copy(
             src_ref=src, dst_ref=dst, send_sem=ss, recv_sem=rs, device_id={"seq": device}, device_id_type=MESH
         )
 
     def ml_to_partner():
-        return remote(half_ml, peer_ml, hsm, hrm, partner)
+        return remote(half_ml, peer_ml, ml_sent, peer_sem.at[0], partner)
 
     def num_to_partner(j):
-        return remote(half_num.at[j], peer_num.at[j], hs.at[j], hr.at[j], partner)
+        return remote(half_num.at[j], peer_num.at[j], rest_sent, peer_sem.at[1], partner)
 
     targets = [0, 1, middle * 2, middle * 2 + 1]
 
     def ml_to_root(i):
-        return remote(chip_ml.at[chip], chip_ml.at[chip], csm.at[i], crm.at[chip], targets[i] * 2 + core)
+        return remote(chip_ml.at[chip], chip_ml.at[chip], ml_sent, ml_sem, targets[i] * 2 + core)
 
     def num_to_root(j, i):
-        return remote(chip_num.at[j, chip], chip_num.at[j, chip], cs.at[j, i], cr.at[j, chip], targets[i] * 2 + core)
-
-    def ml_from_chip(k):
-        slot = (chip + k) % chips
-        return remote(chip_ml.at[slot], chip_ml.at[slot], csm.at[0], crm.at[slot], slot * 2 + core)
-
-    def num_from_chip(j, k):
-        slot = (chip + k) % chips
-        return remote(chip_num.at[j, slot], chip_num.at[j, slot], cs.at[j, 0], cr.at[j, slot], slot * 2 + core)
+        sent = rest_sent if i else first_sent
+        return remote(chip_num.at[j, chip], chip_num.at[j, chip], sent, num_sem.at[j], targets[i] * 2 + core)
 
     def part_of(owner, j):
         return out.at[:, pl.ds(pl.multiple_of(owner * (CHUNKS * span) + j * span, span), span), :]
@@ -226,8 +224,7 @@
         pl.semaphore_wait(barrier, 5)
 
     ml_to_partner().start()
-    for j in range(CHUNKS):
-        v_copy(j).wait()
+    drain(vbuf.at[:CHUNKS], vsem.at[0])
     for j in range(CHUNKS):
         half_num[j] = gather(0, j).astype(jnp.bfloat16)
     for j in range(CHUNKS):
@@ -235,7 +232,7 @@
     k_copy(3).wait()
     own_top = score(1, 1, own_top)
     ml = weigh(1, own_top)
-    ml_to_partner().wait_recv()
+    drain(peer_ml, peer_sem.at[0])
     other = peer_ml[...]
     top = jnp.maximum(ml[0:1], other[0:1])
     mine = jnp.exp2((ml[0:1] - top) * SHIFT)
@@ -244,38 +241,29 @@
     columns = jnp.transpose(jnp.concatenate([mine, theirs, jnp.zeros((6, lanes), jnp.float32)], axis=0))
     for i in range(len(targets)):
         elsewhere(i, lambda: ml_to_root(i).start())
-    for j in range(CHUNKS):
-        v_copy(CHUNKS + j).wait()
+    drain(vbuf.at[CHUNKS:], vsem.at[1])
     numers = [gather(1, j) for j in range(CHUNKS)]
-    for j in range(CHUNKS):
-        num_to_partner(j).wait_recv()
+    drain(peer_num, peer_sem.at[1])
+    for j in range(CHUNKS):
         some = slice(j * block, (j + 1) * block)
         total = numers[j] * columns[some, 0:1] + peer_num[j].astype(jnp.float32) * columns[some, 1:2]
         chip_num[j, chip] = total.astype(jnp.bfloat16)
         elsewhere(0, lambda: num_to_root(j, 0).start())
+    @pl.when(core == 1)
+    def _():
+        elsewhere(0, lambda: drain(chip_num.at[0, :CHUNKS], first_sent))
+
     for j in range(CHUNKS):
         elsewhere(2 + j, lambda: num_to_root(j, 2 + j).start())
-    @pl.when(core == 1)
-    def _():
-        for j in range(CHUNKS):
-            elsewhere(0, lambda: num_to_root(j, 0).wait_send())
-
     for j in range(CHUNKS):
         elsewhere(1, lambda: num_to_root(j, 1).start())
 
     def share(j):
-        yield (0, partner), remote(part_of(core, j), part_of(core, j), fs.at[0], fr.at[core, j], partner)
-        for d in range(2):
-            yield (1 + d, across + d), remote(part_of(core, j), part_of(core, j), fs.at[1 + d], fr.at[core, j], across + d)
-        for g, p in enumerate(guests):
-            for d in range(4):
-                yield (3 + 4 * g + d, p * 4 + d), remote(
-                    part_of(core, j), part_of(core, j), fs.at[3 + 4 * g + d], fr.at[core, j], p * 4 + d
-                )
+        fans = [partner, across, across + 1] + [p * 4 + d for p in guests for d in range(4)]
+        return [remote(part_of(core, j), part_of(core, j), shared, fin, device) for device in fans]
 
     def collect(j, columns):
-        for k in range(1, chips):
-            num_from_chip(j, k).wait_recv()
+        drain(chip_num.at[j, : chips - 1], num_sem.at[j])
         numer = None
         for i in range(chips):
             term = chip_num[j, i].astype(jnp.float32) * columns[j * block : (j + 1) * block, i : i + 1]
@@ -287,8 +275,7 @@
                 out[t, pl.ds(base, tile), :] = attended[e * rows + t * tile : e * rows + (t + 1) * tile]
 
     def factors_of_chips():
-        for k in range(1, chips):
-            ml_from_chip(k).wait_recv()
+        drain(chip_ml.at[: chips - 1], ml_sem)
         maxima = [chip_ml[i][0:1] for i in range(chips)]
         top = functools.reduce(jnp.maximum, maxima)
         factors = [jnp.exp2((m - top) * SHIFT) for m in maxima]
@@ -299,50 +286,48 @@
             factors = factors + [jnp.zeros((pad, lanes), jnp.float32)]
         return jnp.transpose(jnp.concatenate(factors, axis=0))
 
-    def swap(j, owner):
-        return remote(part_of(core, j), part_of(owner, j), ps.at[j], pr.at[j], partner)
-
     @pl.when(first)
     def _():
         columns = factors_of_chips()
         for j in range(CHUNKS):
             collect(j, columns)
-            swap(j, core).start()
-        for j in range(CHUNKS):
-            swap(j, 1 - core).wait_recv()
-        for j in range(CHUNKS):
-            swap(j, core).wait_send()
+            remote(part_of(core, j), part_of(core, j), shared, fin, partner).start()
 
     for j in range(CHUNKS):
         @pl.when(central & (y == j))
         def _():
             collect(j, factors_of_chips())
-            for _, copy in share(j):
+            for copy in share(j):
                 copy.start()
 
-    @pl.when(jnp.logical_not(first))
-    def _():
-        for d in range(2):
-            for j in range(CHUNKS):
-                @pl.when(jnp.logical_not(central & (core == d) & (y == j)))
-                def _():
-                    remote(part_of(d, j), part_of(d, j), fs.at[0], fr.at[d, j], (middle * 2 + j) * 2 + d).wait_recv()
-
-    for j in range(CHUNKS):
-        @pl.when(central & (y == j))
+    def sent(units, sem):
+        drain(kbuf.at[0, : units * block * HD // wide], sem)
+
+    for who, at_roots, others in (
+        (guest, 4, 6), (central, 3, 5), (chip == 0, 3, 6), (chip == 1, 3, 4),
+    ):
+        @pl.when(who)
         def _():
-            for _, copy in share(j):
-                copy.wait_send()
-
-    ml_to_partner().wait_send()
-    for j in range(CHUNKS):
-        num_to_partner(j).wait_send()
-        for i in (0, 1, 2 + j):
-            @pl.when((core == 0) | (i != 0))
-            def _():
-                elsewhere(i, lambda: num_to_root(j, i).wait_send())
-    for i in range(len(targets)):
-        elsewhere(i, lambda: ml_to_root(i).wait_send())
+            drain(chip_ml.at[: 1 + at_roots], ml_sent)
+            sent(others, rest_sent)
+
+    @pl.when(core == 0)
+    def _():
+        elsewhere(0, lambda: drain(chip_num.at[0, :CHUNKS], first_sent))
+
+    @pl.when(first)
+    def _():
+        drain(out.at[:, : CHUNKS * span], fin)
+        sent(CHUNKS, shared)
+
+    @pl.when(central)
+    def _():
+        drain(out.at[:, : 3 * span], fin)
+        sent(3 + 4 * len(guests), shared)
+
+    @pl.when(guest)
+    def _():
+        drain(out, fin)
 
 
 def per_device(n, queries, cache_k, cache_v, context_len, slot_seq, slot_pos):
@@ -380,11 +365,7 @@
             pltpu.VMEM((2, lanes), jnp.float32),
             pltpu.VMEM((CHUNKS, chips, block, HD), jnp.bfloat16),
             pltpu.VMEM((chips, 2, lanes), jnp.float32),
-            dma((4,)), dma((2 * CHUNKS,)), dma((2 * CHUNKS,)),
-            dma((CHUNKS,)), dma(()), dma((CHUNKS,)), dma(()),
-            dma((CHUNKS, 4)), dma((4,)), dma((CHUNKS, chips)), dma((chips,)),
-            dma((CHUNKS,)), dma((CHUNKS,)),
-            dma((4 * chips,)), dma((2, CHUNKS)),
+            dma((4,)), dma((2 * CHUNKS,)), dma((2,)), dma((2,)), dma(()), dma((CHUNKS,)), dma(()),
         ],
         compiler_params=pltpu.CompilerParams(collective_id=0, has_side_effects=True, vmem_limit_bytes=LIMIT),
     )(*[

time: 15.2 us -> 14.3 us (0.941)
  Pallas kernels: 14.4 us -> 13.5 us
    pallas_call x1, Pallas kernels: 14.4 us -> 13.5 us  [per_device(): pl.pallas_call(functools.partial(kernel, n), out_shape=jax.ShapeDtypeStru...]
where the time goes in v6:
time: 14.3 us; the launch traced here: 14.2 us
  Pallas kernels  13.5 us (94%)
  local copies, waits for them, and re-layouts  0.63 us (4%)
    pallas_call x1, Pallas kernels, per_device(): pl.pallas_call(functools.partial(kernel, n), out_shape=jax.ShapeDtypeStru...  13.5 us
    unnamed x1, local copies, waits for them, and re-layouts  0.63 us

profile of v6, /device:TPU:0, one launch (start us, length us, event | category | flops | bytes accessed | tf_op | source)
XLA Modules:
  0.0 14.2 jit_solution(14137392173026682564)
XLA Ops:
  0.0 13.5 %shard_map.64 = bf16[2,128,128]{2,1,0:T(8,128)(2,1)S(1)} custom-call(s32[2]{0:T(128)} %ctx_hbm.1, bf16[2,2,8192]{2,1,0:T(2,128)(2,1)} %q_hbm.1, bf16[2048,1024]{1,0:T(8,128)(2,1)} %k_hbm.1, bf16[2048,1024]{1,0:T(8,128)(2,1)} %v_hbm.1, s32[1,2048]{1,0:T(1,128)} %bitcast.8, s32[1,2048]{1,0:T(1,128)} %bitcast.9), custom_call_target="tpu_custom_call" | custom-call | tf_op jit(solution)/shard_map/pallas_call | solution.py:345
  13.5 0.6 %copy.9 = bf16[2,2,8192]{2,1,0:T(2,128)(2,1)} copy(bf16[2,2,8192]{2,1,0:T(2,128)(2,1)S(1)} %bitcast.7) | data formatting | bytes 131072

commit v7 on v6

--- a/solution.py
+++ b/solution.py
@@ -72,23 +72,25 @@
         columns = pl.ds(pl.multiple_of(first_column(order), wide), wide)
         return pltpu.make_async_copy(k_hbm.at[some, columns], kbuf.at[order, some], ksem.at[i])
 
-    def v_copy(i):
-        order, part = i // CHUNKS, i % CHUNKS
-        columns = pl.ds(pl.multiple_of(first_column(order) + part * width, width), width)
-        return pltpu.make_async_copy(v_hbm.at[:, columns], vbuf.at[i], vsem.at[order])
+    def v_copy(order):
+        columns = pl.ds(pl.multiple_of(first_column(order), wide), wide)
+        return pltpu.make_async_copy(v_hbm.at[:, columns], vbuf.at[order], vsem.at[order])
 
     def load_k(i, carry):
         k_copy(i).start()
         return carry
 
-    def load_v(i, carry):
-        v_copy(i).start()
+    def load_v(order, carry):
+        v_copy(order).start()
+
+        @pl.when(order == 0)
+        def _():
+            k_copy(2 * CHUNKS - 1).start()
+
         return carry
 
-    lax.fori_loop(0, 3, load_k, 0)
+    lax.fori_loop(0, 2 * CHUNKS - 1, load_k, 0)
     lax.fori_loop(0, 2, load_v, 0)
-    k_copy(3).start()
-    lax.fori_loop(2, 4, load_v, 0)
 
     greet(partner)
 
@@ -164,7 +166,7 @@
             [
                 jnp.dot(
                     pbuf[order, (j * heads_each + e) * rows : (j * heads_each + e + 1) * rows, :],
-                    vbuf[order * CHUNKS + j, :, e * HD : (e + 1) * HD], preferred_element_type=jnp.float32,
+                    vbuf[order, :, j * width + e * HD : j * width + (e + 1) * HD], preferred_element_type=jnp.float32,
                 )
                 for e in range(heads_each)
             ],
@@ -188,13 +190,14 @@
         return remote(half_num.at[j], peer_num.at[j], rest_sent, peer_sem.at[1], partner)
 
     targets = [0, 1, middle * 2, middle * 2 + 1]
+    late = plane // (planes - 1)
 
     def ml_to_root(i):
         return remote(chip_ml.at[chip], chip_ml.at[chip], ml_sent, ml_sem, targets[i] * 2 + core)
 
     def num_to_root(j, i):
         sent = rest_sent if i else first_sent
-        return remote(chip_num.at[j, chip], chip_num.at[j, chip], sent, num_sem.at[j], targets[i] * 2 + core)
+        return remote(chip_num.at[j, chip], chip_num.at[j, chip], sent, num_sem.at[late * CHUNKS + j], targets[i] * 2 + core)
 
     def part_of(owner, j):
         return out.at[:, pl.ds(pl.multiple_of(owner * (CHUNKS * span) + j * span, span), span), :]
@@ -224,7 +227,7 @@
         pl.semaphore_wait(barrier, 5)
 
     ml_to_partner().start()
-    drain(vbuf.at[:CHUNKS], vsem.at[0])
+    v_copy(0).wait()
     for j in range(CHUNKS):
         half_num[j] = gather(0, j).astype(jnp.bfloat16)
     for j in range(CHUNKS):
@@ -241,7 +244,7 @@
     columns = jnp.transpose(jnp.concatenate([mine, theirs, jnp.zeros((6, lanes), jnp.float32)], axis=0))
     for i in range(len(targets)):
         elsewhere(i, lambda: ml_to_root(i).start())
-    drain(vbuf.at[CHUNKS:], vsem.at[1])
+    v_copy(1).wait()
     numers = [gather(1, j) for j in range(CHUNKS)]
     drain(peer_num, peer_sem.at[1])
     for j in range(CHUNKS):
@@ -262,13 +265,19 @@
         fans = [partner, across, across + 1] + [p * 4 + d for p in guests for d in range(4)]
         return [remote(part_of(core, j), part_of(core, j), shared, fin, device) for device in fans]
 
-    def collect(j, columns):
-        drain(chip_num.at[j, : chips - 1], num_sem.at[j])
-        numer = None
-        for i in range(chips):
+    def add_up(j, columns, some, numer):
+        for i in some:
             term = chip_num[j, i].astype(jnp.float32) * columns[j * block : (j + 1) * block, i : i + 1]
             numer = term if numer is None else numer + term
-        attended = numer.astype(jnp.bfloat16)
+        return numer
+
+    def gather_early(j, columns):
+        drain(chip_num.at[j, : chips - 3], num_sem.at[j])
+        return add_up(j, columns, range(chips - 2), None)
+
+    def collect(j, columns, numer):
+        drain(chip_num.at[j, :2], num_sem.at[CHUNKS + j])
+        attended = add_up(j, columns, range(chips - 2, chips), numer).astype(jnp.bfloat16)
         for e in range(heads_each):
             for t in range(2):
                 base = pl.multiple_of(core * (CHUNKS * span) + j * span + e * tile, tile)
@@ -289,14 +298,16 @@
     @pl.when(first)
     def _():
         columns = factors_of_chips()
+        early = [gather_early(j, columns) for j in range(CHUNKS)]
         for j in range(CHUNKS):
-            collect(j, columns)
+            collect(j, columns, early[j])
             remote(part_of(core, j), part_of(core, j), shared, fin, partner).start()
 
     for j in range(CHUNKS):
         @pl.when(central & (y == j))
         def _():
-            collect(j, factors_of_chips())
+            columns = factors_of_chips()
+            collect(j, columns, gather_early(j, columns))
             for copy in share(j):
                 copy.start()
 
@@ -353,7 +364,7 @@
             pltpu.VMEM((1, slots), jnp.int32),
             pltpu.VMEM((1, slots), jnp.int32),
             pltpu.VMEM((2, slots, heads_half * HD), jnp.bfloat16),
-            pltpu.VMEM((2 * CHUNKS, slots, heads_half * HD // CHUNKS), jnp.bfloat16),
+            pltpu.VMEM((2, slots, heads_half * HD), jnp.bfloat16),
             pltpu.VMEM((KVH * rows, HD), jnp.float32),
             pltpu.VMEM((2, heads_half * HD, lanes), jnp.bfloat16),
             pltpu.VMEM((slots, lanes), jnp.float32),
@@ -365,7 +376,7 @@
             pltpu.VMEM((2, lanes), jnp.float32),
             pltpu.VMEM((CHUNKS, chips, block, HD), jnp.bfloat16),
             pltpu.VMEM((chips, 2, lanes), jnp.float32),
-            dma((4,)), dma((2 * CHUNKS,)), dma((2,)), dma((2,)), dma(()), dma((CHUNKS,)), dma(()),
+            dma((4,)), dma((2 * CHUNKS,)), dma((2,)), dma((2,)), dma(()), dma((2 * CHUNKS,)), dma(()),
         ],
         compiler_params=pltpu.CompilerParams(collective_id=0, has_side_effects=True, vmem_limit_bytes=LIMIT),
     )(*[

time: 14.3 us -> 14.2 us (level)
  no operation moved by 1% of the time
where the time goes in v7:
time: 14.2 us; the launch traced here: 14.1 us
  Pallas kernels  13.5 us (95%)
  local copies, waits for them, and re-layouts  0.63 us (4%)
    pallas_call x1, Pallas kernels, per_device(): pl.pallas_call(functools.partial(kernel, n), out_shape=jax.ShapeDtypeStru...  13.5 us
    unnamed x1, local copies, waits for them, and re-layouts  0.63 us

profile of v7, /device:TPU:0, one launch (start us, length us, event | category | flops | bytes accessed | tf_op | source)
XLA Modules:
  0.0 14.1 jit_solution(6823427265052775216)
XLA Ops:
  0.0 13.5 %shard_map.64 = bf16[2,128,128]{2,1,0:T(8,128)(2,1)S(1)} custom-call(s32[2]{0:T(128)} %ctx_hbm.1, bf16[2,2,8192]{2,1,0:T(2,128)(2,1)} %q_hbm.1, bf16[2048,1024]{1,0:T(8,128)(2,1)} %k_hbm.1, bf16[2048,1024]{1,0:T(8,128)(2,1)} %v_hbm.1, s32[1,2048]{1,0:T(1,128)} %bitcast.8, s32[1,2048]{1,0:T(1,128)} %bitcast.9), custom_call_target="tpu_custom_call" | custom-call | tf_op jit(solution)/shard_map/pallas_call | solution.py:356
  13.5 0.6 %copy.9 = bf16[2,2,8192]{2,1,0:T(2,128)(2,1)} copy(bf16[2,2,8192]{2,1,0:T(2,128)(2,1)S(1)} %bitcast.7) | data formatting | bytes 131072

commit v8 on v7

--- a/solution.py
+++ b/solution.py
@@ -19,7 +19,7 @@
 
 def kernel(
     n, ctx_hbm, q_hbm, k_hbm, v_hbm, seq_hbm, pos_hbm, out,
-    ctx, q_ref, seq_ref, pos_ref, kbuf, vbuf, qf, qt, bias, sbuf, pbuf,
+    ctx, q_ref, slot_ref, kbuf, vbuf, qf, qt, bias, sbuf, pbuf,
     half_num, half_ml, peer_num, peer_ml, chip_num, chip_ml,
     isem, ksem, vsem, peer_sem, ml_sem, num_sem, fin,
 ):
@@ -56,8 +56,9 @@
     def greet(device):
         pl.semaphore_signal(barrier, inc=1, device_id={"seq": device}, device_id_type=MESH)
 
+    seq_ref, pos_ref = slot_ref.at[0], slot_ref.at[1]
     inputs = []
-    for i, (src, dst) in enumerate(((q_hbm, q_ref), (seq_hbm, seq_ref), (pos_hbm, pos_ref), (ctx_hbm, ctx))):
+    for i, src, dst in ((0, q_hbm, q_ref), (1, seq_hbm, seq_ref), (1, pos_hbm, pos_ref), (2, ctx_hbm, ctx)):
         copy = pltpu.make_async_copy(src, dst, isem.at[i])
         copy.start()
         inputs.append(copy)
@@ -108,8 +109,9 @@
         for d in range(4):
             greet(middle * 4 + d)
 
-    for copy in inputs:
-        copy.wait()
+    inputs[0].wait()
+    pltpu.make_async_copy(slot_ref, slot_ref, isem.at[1]).wait()
+    inputs[3].wait()
 
     for t in range(2):
         for head in range(KVH * group):
@@ -176,7 +178,7 @@
     def drain(ref, sem):
         pltpu.make_async_copy(ref, ref, sem).wait()
 
-    rest_sent, ml_sent, first_sent, shared = (isem.at[i] for i in range(4))
+    rest_sent, ml_sent, first_sent = (isem.at[i] for i in range(3))
 
     def remote(src, dst, ss, rs, device):
         return pltpu.make_async_remote_copy(
@@ -197,7 +199,7 @@
 
     def num_to_root(j, i):
         sent = rest_sent if i else first_sent
-        return remote(chip_num.at[j, chip], chip_num.at[j, chip], sent, num_sem.at[late * CHUNKS + j], targets[i] * 2 + core)
+        return remote(chip_num.at[j, chip], chip_num.at[j, chip], sent, num_sem.at[late * (1 + j)], targets[i] * 2 + core)
 
     def part_of(owner, j):
         return out.at[:, pl.ds(pl.multiple_of(owner * (CHUNKS * span) + j * span, span), span), :]
@@ -258,12 +260,16 @@
 
     for j in range(CHUNKS):
         elsewhere(2 + j, lambda: num_to_root(j, 2 + j).start())
+    @pl.when(core == 0)
+    def _():
+        elsewhere(0, lambda: drain(chip_num.at[0, :CHUNKS], first_sent))
+
     for j in range(CHUNKS):
         elsewhere(1, lambda: num_to_root(j, 1).start())
 
     def share(j):
         fans = [partner, across, across + 1] + [p * 4 + d for p in guests for d in range(4)]
-        return [remote(part_of(core, j), part_of(core, j), shared, fin, device) for device in fans]
+        return [remote(part_of(core, j), part_of(core, j), rest_sent, fin, device) for device in fans]
 
     def add_up(j, columns, some, numer):
         for i in some:
@@ -272,11 +278,10 @@
         return numer
 
     def gather_early(j, columns):
-        drain(chip_num.at[j, : chips - 3], num_sem.at[j])
         return add_up(j, columns, range(chips - 2), None)
 
     def collect(j, columns, numer):
-        drain(chip_num.at[j, :2], num_sem.at[CHUNKS + j])
+        drain(chip_num.at[j, :2], num_sem.at[1 + j])
         attended = add_up(j, columns, range(chips - 2, chips), numer).astype(jnp.bfloat16)
         for e in range(heads_each):
             for t in range(2):
@@ -298,15 +303,17 @@
     @pl.when(first)
     def _():
         columns = factors_of_chips()
+        drain(chip_num.at[:, : chips - 3], num_sem.at[0])
         early = [gather_early(j, columns) for j in range(CHUNKS)]
         for j in range(CHUNKS):
             collect(j, columns, early[j])
-            remote(part_of(core, j), part_of(core, j), shared, fin, partner).start()
+            remote(part_of(core, j), part_of(core, j), rest_sent, fin, partner).start()
 
     for j in range(CHUNKS):
         @pl.when(central & (y == j))
         def _():
             columns = factors_of_chips()
+            drain(chip_num.at[j, : chips - 3], num_sem.at[0])
             collect(j, columns, gather_early(j, columns))
             for copy in share(j):
                 copy.start()
@@ -315,26 +322,20 @@
         drain(kbuf.at[0, : units * block * HD // wide], sem)
 
     for who, at_roots, others in (
-        (guest, 4, 6), (central, 3, 5), (chip == 0, 3, 6), (chip == 1, 3, 4),
+        (guest, 4, 6), (central, 3, 8 + 4 * len(guests)), (chip == 0, 3, 6 + CHUNKS), (chip == 1, 3, 4 + CHUNKS),
     ):
         @pl.when(who)
         def _():
             drain(chip_ml.at[: 1 + at_roots], ml_sent)
             sent(others, rest_sent)
 
-    @pl.when(core == 0)
-    def _():
-        elsewhere(0, lambda: drain(chip_num.at[0, :CHUNKS], first_sent))
-
     @pl.when(first)
     def _():
         drain(out.at[:, : CHUNKS * span], fin)
-        sent(CHUNKS, shared)
 
     @pl.when(central)
     def _():
         drain(out.at[:, : 3 * span], fin)
-        sent(3 + 4 * len(guests), shared)
 
     @pl.when(guest)
     def _():
@@ -361,8 +362,7 @@
         scratch_shapes=[
             pltpu.SMEM((seqs,), jnp.int32),
             pltpu.VMEM(queries.shape, jnp.bfloat16),
-            pltpu.VMEM((1, slots), jnp.int32),
-            pltpu.VMEM((1, slots), jnp.int32),
+            pltpu.VMEM((2, 1, slots), jnp.int32),
             pltpu.VMEM((2, slots, heads_half * HD), jnp.bfloat16),
             pltpu.VMEM((2, slots, heads_half * HD), jnp.bfloat16),
             pltpu.VMEM((KVH * rows, HD), jnp.float32),
@@ -376,7 +376,7 @@
             pltpu.VMEM((2, lanes), jnp.float32),
             pltpu.VMEM((CHUNKS, chips, block, HD), jnp.bfloat16),
             pltpu.VMEM((chips, 2, lanes), jnp.float32),
-            dma((4,)), dma((2 * CHUNKS,)), dma((2,)), dma((2,)), dma(()), dma((2 * CHUNKS,)), dma(()),
+            dma((3,)), dma((2 * CHUNKS,)), dma((2,)), dma((2,)), dma(()), dma((1 + CHUNKS,)), dma(()),
         ],
         compiler_params=pltpu.CompilerParams(collective_id=0, has_side_effects=True, vmem_limit_bytes=LIMIT),
     )(*[

time: 14.2 us -> 14.2 us (level)
  no operation moved by 1% of the time
where the time goes in v8:
time: 14.2 us; the launch traced here: 14.1 us
  Pallas kernels  13.4 us (94%)
  local copies, waits for them, and re-layouts  0.63 us (4%)
    pallas_call x1, Pallas kernels, per_device(): pl.pallas_call(functools.partial(kernel, n), out_shape=jax.ShapeDtypeStru...  13.4 us
    unnamed x1, local copies, waits for them, and re-layouts  0.63 us

profile of v8, /device:TPU:0, one launch (start us, length us, event | category | flops | bytes accessed | tf_op | source)
XLA Modules:
  0.0 14.1 jit_solution(16461972989847070849)
XLA Ops:
  0.0 13.4 %shard_map.64 = bf16[2,128,128]{2,1,0:T(8,128)(2,1)S(1)} custom-call(s32[2]{0:T(128)} %ctx_hbm.1, bf16[2,2,8192]{2,1,0:T(2,128)(2,1)} %q_hbm.1, bf16[2048,1024]{1,0:T(8,128)(2,1)} %k_hbm.1, bf16[2048,1024]{1,0:T(8,128)(2,1)} %v_hbm.1, s32[1,2048]{1,0:T(1,128)} %bitcast.8, s32[1,2048]{1,0:T(1,128)} %bitcast.9), custom_call_target="tpu_custom_call" | custom-call | tf_op jit(solution)/shard_map/pallas_call | solution.py:357
  13.4 0.6 %copy.9 = bf16[2,2,8192]{2,1,0:T(2,128)(2,1)} copy(bf16[2,2,8192]{2,1,0:T(2,128)(2,1)S(1)} %bitcast.7) | data formatting | bytes 131072

commit v9 on v8

--- a/solution.py
+++ b/solution.py
@@ -212,10 +212,10 @@
     k_copy(0).wait()
     top = score(0, 0, None)
     k_copy(1).wait()
+    k_copy(2).wait()
     top = score(0, 1, top)
-    k_copy(2).wait()
+    own_top = score(1, 0, None)
     half_ml[...] = weigh(0, top)
-    own_top = score(1, 0, None)
     @pl.when(first)
     def _():
         pl.semaphore_wait(barrier, 4)

time: 14.2 us -> 14.1 us (level)
  no operation moved by 1% of the time
where the time goes in v9:
time: 14.1 us; the launch traced here: 14 us
  Pallas kernels  13.3 us (94%)
  local copies, waits for them, and re-layouts  0.63 us (4%)
    pallas_call x1, Pallas kernels, per_device(): pl.pallas_call(functools.partial(kernel, n), out_shape=jax.ShapeDtypeStru...  13.3 us
    unnamed x1, local copies, waits for them, and re-layouts  0.63 us

profile of v9, /device:TPU:0, one launch (start us, length us, event | category | flops | bytes accessed | tf_op | source)
XLA Modules:
  0.0 14.0 jit_solution(10063358777548843710)
XLA Ops:
  0.0 13.3 %shard_map.64 = bf16[2,128,128]{2,1,0:T(8,128)(2,1)S(1)} custom-call(s32[2]{0:T(128)} %ctx_hbm.1, bf16[2,2,8192]{2,1,0:T(2,128)(2,1)} %q_hbm.1, bf16[2048,1024]{1,0:T(8,128)(2,1)} %k_hbm.1, bf16[2048,1024]{1,0:T(8,128)(2,1)} %v_hbm.1, s32[1,2048]{1,0:T(1,128)} %bitcast.8, s32[1,2048]{1,0:T(1,128)} %bitcast.9), custom_call_target="tpu_custom_call" | custom-call | tf_op jit(solution)/shard_map/pallas_call | solution.py:357
  13.4 0.6 %copy.9 = bf16[2,2,8192]{2,1,0:T(2,128)(2,1)} copy(bf16[2,2,8192]{2,1,0:T(2,128)(2,1)S(1)} %bitcast.7) | data formatting | bytes 131072
